TPU v7x, 32 devices: a whole 2x2x4 slice. The times are simulated.
32 devices in a mesh: fsdp: 8 (over z, y), tensor: 4 (over x, core).
Axes of the slice: x: 2, y: 2, z: 4, core: 2. Of those that a mesh axis runs over, the one named last changes fastest.
Arguments:
- block_input: bfloat16 [16, 197, 768], P('fsdp'), may hold values from -6 to 6
- output_grad: bfloat16 [16, 197, 768], P('fsdp'), may hold values from -6 to 6
- live_images: int32 [16], P('fsdp'), may hold values from 0 to 1, as said below
- w_qkv: float32 [768, 3, 768], P('fsdp', None, 'tensor'), may hold values from -6 to 6
- w_out: float32 [768, 768], P('tensor', 'fsdp'), may hold values from -0.625 to 0.625
- w_fc1: float32 [768, 3072], P('fsdp', 'tensor'), may hold values from -0.21875 to 0.21875
- w_fc2: float32 [3072, 768], P('tensor', 'fsdp'), may hold values from -0.109375 to 0.109375
- qv_bias: float32 [2, 12, 64], P(None, 'tensor', 'fsdp'), may hold values from -1.2 to 1.2
- fc1_bias: float32 [48, 64], P('tensor', 'fsdp'), may hold values from -1.2 to 1.2
- norm_vec: float32 [6, 768], P(None, 'fsdp'), may hold values from -0.9 to 1.5
- mom_qkv: float32 [2, 768, 3, 768], P(None, 'fsdp', None, 'tensor'), may hold values from -5.0528408 to 5.0528408, as said below
- mom_out: float32 [2, 768, 768], P(None, 'tensor', 'fsdp'), may hold values from -5.0528408 to 5.0528408, as said below
- mom_fc1: float32 [2, 768, 3072], P(None, 'fsdp', 'tensor'), may hold values from -5.0528408 to 5.0528408, as said below
- mom_fc2: float32 [2, 3072, 768], P(None, 'tensor', 'fsdp'), may hold values from -5.0528408 to 5.0528408, as said below
- mom_qvb: float32 [2, 2, 12, 64], P(None, None, 'tensor', 'fsdp'), may hold values from -5.0528408 to 5.0528408, as said below
- mom_fc1b: float32 [2, 48, 64], P(None, 'tensor', 'fsdp'), may hold values from -5.0528408 to 5.0528408, as said below
- mom_vec: float32 [2, 6, 768], P(None, None, 'fsdp'), may hold values from -5.0528408 to 5.0528408, as said below
Outputs:
- block_output: bfloat16 [16, 197, 768], P('fsdp')
- input_grad: float32 [16, 197, 768], P('fsdp')
- grad_qkv: float32 [768, 3, 768], P('fsdp', None, 'tensor')
- grad_out: float32 [768, 768], P('tensor', 'fsdp')
- grad_fc1: float32 [768, 3072], P('fsdp', 'tensor')
- grad_fc2: float32 [3072, 768], P('tensor', 'fsdp')
- grad_qvb: float32 [2, 12, 64], P(None, 'tensor', 'fsdp')
- grad_fc1b: float32 [48, 64], P('tensor', 'fsdp')
- grad_vec: float32 [6, 768], P(None, 'fsdp')
- new_qkv: float32 [768, 3, 768], P('fsdp', None, 'tensor')
- new_out: float32 [768, 768], P('tensor', 'fsdp')
- new_fc1: float32 [768, 3072], P('fsdp', 'tensor')
- new_fc2: float32 [3072, 768], P('tensor', 'fsdp')
- new_qvb: float32 [2, 12, 64], P(None, 'tensor', 'fsdp')
- new_fc1b: float32 [48, 64], P('tensor', 'fsdp')
- new_vec: float32 [6, 768], P(None, 'fsdp')
- newmom_qkv: float32 [2, 768, 3, 768], P(None, 'fsdp', None, 'tensor')
- newmom_out: float32 [2, 768, 768], P(None, 'tensor', 'fsdp')
- newmom_fc1: float32 [2, 768, 3072], P(None, 'fsdp', 'tensor')
- newmom_fc2: float32 [2, 3072, 768], P(None, 'tensor', 'fsdp')
- newmom_qvb: float32 [2, 2, 12, 64], P(None, None, 'tensor', 'fsdp')
- newmom_fc1b: float32 [2, 48, 64], P(None, 'tensor', 'fsdp')
- newmom_vec: float32 [2, 6, 768], P(None, None, 'fsdp')
Inputs may be any that keep to these rules, and one draw needn't show every extreme that they name: `live_images`: in each aligned block of 2 slots (those of one index of fsdp) either all images are live or exactly one slot is empty; blocks of both kinds occur in every draw. `mom_qkv`: the second moments are positive. `mom_out`: the second moments are positive. `mom_fc1`: the second moments are positive. `mom_fc2`: the second moments are positive. `mom_qvb`: the second moments are positive. `mom_fc1b`: the second moments are positive. `mom_vec`: the second moments are positive.
All inputs are finite; a program needn't handle non-finite values.
Results may differ from a plain program's by a relative error of at most 0.017.
Values may be sent and summed in bfloat16 or wider, within the bound.
A program may use at most 64 MiB of HBM per device.

v0:
```python
import jax
import jax.numpy as jnp
from jax import lax
from jax.sharding import PartitionSpec as P

HD = 64


epsilon = 1e-06
sqrt_half = 0.7071067811865476
inv_root = 0.3989422804014327
corr_one = 1.0 - 0.9**3
corr_two = 1.0 - 0.999**3


def norm_forward(values, gain, shift):
    center = values - jnp.mean(values, axis=-1, keepdims=True)
    variance = jnp.mean(center * center, axis=-1, keepdims=True)
    scale = lax.rsqrt(variance + epsilon)
    normed = center * scale
    return (normed * gain + shift, normed, scale)


def norm_backward(upstream, normed, scale, gain):
    scaled = upstream * gain
    return scale * (
        scaled
        - jnp.mean(scaled, axis=-1, keepdims=True)
        - normed * jnp.mean(scaled * normed, axis=-1, keepdims=True)
    )


def gelu_slope(pre_act):
    return (
        0.5 * (1.0 + lax.erf(pre_act * sqrt_half))
        + pre_act * jnp.exp(-0.5 * pre_act * pre_act) * inv_root
    )


def attend(queries, key_rows, value_rows):
    scores = (
        jnp.einsum("bqhe,bkhe->bhqk", queries, key_rows, preferred_element_type=jnp.float32) * 0.125
    )
    logsum = jax.nn.logsumexp(scores, axis=-1, keepdims=True)
    probs = jnp.exp(scores - logsum).astype(jnp.bfloat16)
    mixed = jnp.einsum("bhqk,bkhe->bqhe", probs, value_rows, preferred_element_type=jnp.float32)
    return (mixed.astype(jnp.bfloat16), logsum)


def attend_back(queries, key_rows, value_rows, logsum, upstream):
    scores = (
        jnp.einsum("bqhe,bkhe->bhqk", queries, key_rows, preferred_element_type=jnp.float32) * 0.125
    )
    probs = jnp.exp(scores - logsum)
    probs_low = probs.astype(jnp.bfloat16)
    dprobs = jnp.einsum("bqhe,bkhe->bhqk", upstream, value_rows, preferred_element_type=jnp.float32)
    dscore = (probs * (dprobs - jnp.sum(probs * dprobs, axis=-1, keepdims=True))).astype(
        jnp.bfloat16
    )
    dquery = 0.125 * jnp.einsum(
        "bhqk,bkhe->bqhe", dscore, key_rows, preferred_element_type=jnp.float32
    )
    dkey = 0.125 * jnp.einsum(
        "bhqk,bqhe->bkhe", dscore, queries, preferred_element_type=jnp.float32
    )
    dvalue = jnp.einsum("bhqk,bqhe->bkhe", probs_low, upstream, preferred_element_type=jnp.float32)
    return (dquery, dkey, dvalue)


def adamw(param, grad, moments):
    first = 0.9 * moments[0] + 0.1 * grad
    second = 0.999 * moments[1] + 0.001 * grad * grad
    fresh = param - 0.004 * (
        first / corr_one / (jnp.sqrt(second / corr_two) + 1e-08) + 0.05 * param
    )
    return (fresh, jnp.stack([first, second]))


def on_device(
    block_input,
    output_grad,
    live_images,
    w_qkv,
    w_out,
    w_fc1,
    w_fc2,
    qv_bias,
    fc1_bias,
    norm_vec,
    mom_qkv,
    mom_out,
    mom_fc1,
    mom_fc2,
    mom_qvb,
    mom_fc1b,
    mom_vec,
):
    low = jnp.bfloat16
    images, seqlen, width = block_input.shape
    rows = images * seqlen
    inward, outward, widen, narrow, heads_bias, hidden_bias, norm_rows = (
        lax.all_gather(w_qkv.astype(low), "fsdp", axis=0, tiled=True),
        lax.all_gather(w_out.astype(low), "fsdp", axis=1, tiled=True),
        lax.all_gather(w_fc1.astype(low), "fsdp", axis=0, tiled=True),
        lax.all_gather(w_fc2.astype(low), "fsdp", axis=1, tiled=True),
        lax.all_gather(qv_bias.astype(low), "fsdp", axis=2, tiled=True),
        lax.all_gather(fc1_bias.astype(low), "fsdp", axis=1, tiled=True),
        lax.all_gather(norm_vec.astype(low), "fsdp", axis=1, tiled=True),
    )
    local_feat = inward.shape[2]
    heads_here = local_feat // HD
    vecf = norm_rows.astype(jnp.float32)
    flat = block_input.astype(jnp.float32).reshape(rows, width)
    first_norm, unit_one, scale_one = norm_forward(flat, vecf[0], vecf[1])
    normed_one = first_norm.astype(low)
    projected = jnp.einsum("nd,dcj->ncj", normed_one, inward, preferred_element_type=jnp.float32)
    biasf = heads_bias.astype(jnp.float32).reshape(2, local_feat)
    shifts = jnp.stack([biasf[0], jnp.zeros_like(biasf[0]), biasf[1]])
    triple = (projected + shifts).astype(low).reshape(images, seqlen, 3, heads_here, HD)
    queries = triple[:, :, 0]
    key_rows = triple[:, :, 1]
    value_rows = triple[:, :, 2]
    mixed, logsum = attend(queries, key_rows, value_rows)
    attn_rows = mixed.reshape(rows, local_feat)
    attn_term = jnp.dot(attn_rows, outward, preferred_element_type=jnp.float32).astype(low)
    attn_total = lax.psum(attn_term, "tensor").astype(jnp.float32)
    resid = flat + attn_total + vecf[4]
    second_norm, unit_two, scale_two = norm_forward(resid, vecf[2], vecf[3])
    normed_two = second_norm.astype(low)
    pre_act = jnp.dot(normed_two, widen, preferred_element_type=jnp.float32) + hidden_bias.astype(
        jnp.float32
    ).reshape(-1)
    activ = jax.nn.gelu(pre_act, approximate=False).astype(low)
    mlp_term = jnp.dot(activ, narrow, preferred_element_type=jnp.float32).astype(low)
    mlp_total = lax.psum(mlp_term, "tensor").astype(jnp.float32)
    row_mask = jnp.broadcast_to(live_images.astype(jnp.float32)[:, None], (images, seqlen)).reshape(
        rows, 1
    )
    block_output = (
        (row_mask * (resid + mlp_total + vecf[5])).astype(low).reshape(images, seqlen, width)
    )
    inward, outward, widen, narrow, norm_rows = (
        lax.all_gather(w_qkv.astype(low), "fsdp", axis=0, tiled=True),
        lax.all_gather(w_out.astype(low), "fsdp", axis=1, tiled=True),
        lax.all_gather(w_fc1.astype(low), "fsdp", axis=0, tiled=True),
        lax.all_gather(w_fc2.astype(low), "fsdp", axis=1, tiled=True),
        lax.all_gather(norm_vec.astype(low), "fsdp", axis=1, tiled=True),
    )
    vecf = norm_rows.astype(jnp.float32)
    grad_flat = output_grad.astype(jnp.float32).reshape(rows, width) * row_mask
    grad_low = grad_flat.astype(low)
    grad_narrow = jnp.einsum("nf,nd->fd", activ, grad_low, preferred_element_type=jnp.float32)
    delta_act = jnp.einsum("nd,fd->nf", grad_low, narrow, preferred_element_type=jnp.float32)
    delta_pre = delta_act * gelu_slope(pre_act)
    delta_pre_low = delta_pre.astype(low)
    grad_hidden = jnp.sum(delta_pre, axis=0).reshape(hidden_bias.shape)
    grad_widen = jnp.einsum(
        "nd,nf->df", normed_two, delta_pre_low, preferred_element_type=jnp.float32
    )
    two_term = jnp.einsum(
        "nf,df->nd", delta_pre_low, widen, preferred_element_type=jnp.float32
    ).astype(low)
    delta_two = lax.psum(two_term, "tensor").astype(jnp.float32)
    delta_resid = grad_flat + norm_backward(delta_two, unit_two, scale_two, vecf[2])
    delta_resid_low = delta_resid.astype(low)
    grad_outward = jnp.einsum(
        "nj,nd->jd", attn_rows, delta_resid_low, preferred_element_type=jnp.float32
    )
    delta_mixed = jnp.einsum(
        "nd,jd->nj", delta_resid_low, outward, preferred_element_type=jnp.float32
    )
    delta_mixed = delta_mixed.astype(low).reshape(images, seqlen, heads_here, HD)
    delta_query, delta_key, delta_value = attend_back(
        queries, key_rows, value_rows, logsum, delta_mixed
    )
    delta_triple = jnp.stack([delta_query, delta_key, delta_value], axis=2).reshape(
        rows, 3, local_feat
    )
    grad_heads = jnp.stack(
        [jnp.sum(delta_triple[:, 0], axis=0), jnp.sum(delta_triple[:, 2], axis=0)]
    ).reshape(2, heads_here, HD)
    triple_low = delta_triple.astype(low)
    grad_inward = jnp.einsum(
        "nd,ncj->dcj", normed_one, triple_low, preferred_element_type=jnp.float32
    )
    one_term = jnp.einsum(
        "ncj,dcj->nd", triple_low, inward, preferred_element_type=jnp.float32
    ).astype(low)
    delta_one = lax.psum(one_term, "tensor").astype(jnp.float32)
    input_grad = (delta_resid + norm_backward(delta_one, unit_one, scale_one, vecf[0])).reshape(
        images, seqlen, width
    )
    grad_rows_vec = jnp.stack(
        [
            jnp.sum(delta_one * unit_one, axis=0),
            jnp.sum(delta_one, axis=0),
            jnp.sum(delta_two * unit_two, axis=0),
            jnp.sum(delta_two, axis=0),
            jnp.sum(delta_resid, axis=0),
            jnp.sum(grad_flat, axis=0),
        ]
    )
    owned = (
        lax.psum_scatter(grad_inward, "fsdp", scatter_dimension=0, tiled=True),
        lax.psum_scatter(grad_outward, "fsdp", scatter_dimension=1, tiled=True),
        lax.psum_scatter(grad_widen, "fsdp", scatter_dimension=0, tiled=True),
        lax.psum_scatter(grad_narrow, "fsdp", scatter_dimension=1, tiled=True),
        lax.psum_scatter(grad_heads, "fsdp", scatter_dimension=2, tiled=True),
        lax.psum_scatter(grad_hidden, "fsdp", scatter_dimension=1, tiled=True),
        lax.psum_scatter(grad_rows_vec, "fsdp", scatter_dimension=1, tiled=True),
    )
    params = (w_qkv, w_out, w_fc1, w_fc2, qv_bias, fc1_bias, norm_vec)
    moments = (mom_qkv, mom_out, mom_fc1, mom_fc2, mom_qvb, mom_fc1b, mom_vec)
    stepped = [adamw(param, grad, moment) for param, grad, moment in zip(params, owned, moments)]
    return (
        (block_output, input_grad)
        + tuple(owned)
        + tuple((entry[0] for entry in stepped))
        + tuple((entry[1] for entry in stepped))
    )


def solution(mesh):
    return jax.shard_map(
        on_device,
        mesh=mesh,
        in_specs=(
            P("fsdp", None, None),
            P("fsdp", None, None),
            P("fsdp"),
            P("fsdp", None, "tensor"),
            P("tensor", "fsdp"),
            P("fsdp", "tensor"),
            P("tensor", "fsdp"),
            P(None, "tensor", "fsdp"),
            P("tensor", "fsdp"),
            P(None, "fsdp"),
            P(None, "fsdp", None, "tensor"),
            P(None, "tensor", "fsdp"),
            P(None, "fsdp", "tensor"),
            P(None, "tensor", "fsdp"),
            P(None, None, "tensor", "fsdp"),
            P(None, "tensor", "fsdp"),
            P(None, None, "fsdp"),
        ),
        out_specs=(
            P("fsdp", None, None),
            P("fsdp", None, None),
            P("fsdp", None, "tensor"),
            P("tensor", "fsdp"),
            P("fsdp", "tensor"),
            P("tensor", "fsdp"),
            P(None, "tensor", "fsdp"),
            P("tensor", "fsdp"),
            P(None, "fsdp"),
            P("fsdp", None, "tensor"),
            P("tensor", "fsdp"),
            P("fsdp", "tensor"),
            P("tensor", "fsdp"),
            P(None, "tensor", "fsdp"),
            P("tensor", "fsdp"),
            P(None, "fsdp"),
            P(None, "fsdp", None, "tensor"),
            P(None, "tensor", "fsdp"),
            P(None, "fsdp", "tensor"),
            P(None, "tensor", "fsdp"),
            P(None, None, "tensor", "fsdp"),
            P(None, "tensor", "fsdp"),
            P(None, None, "fsdp"),
        ),
        check_vma=False,
    )
```

profile of v0, /device:TPU:0, one launch (start us, length us, event | category | flops | bytes accessed | tf_op | source)
XLA Modules:
  0.0 693.3 jit_solution(13144011146463214743)
XLA Ops:
  11.1 27.9 %all-gather = bf16[8,96,6]{1,2,0:T(8,128)(2,1)S(1)} all-gather(bf16[1,96,6]{1,2,0:T(8,128)(2,1)S(1)} %convert_bitcast_fusion), channel_id=1, replica_groups=mesh['fsdp'=8,'tensor'=4] {'fsdp'}, dimensions={0}, use_global_device_ids=true | all-gather | bytes 10368 | tf_op jit(solution)/shard_map/all_gather | solution.py:108
  40.9 35.5 %all_gather.27 = bf16[768,3,192]{2,1,0:T(4,128)(2,1)S(1)} all-gather(bf16[96,3,192]{2,1,0:T(4,128)(2,1)S(1)} %copy.167), channel_id=1, replica_groups=mesh['fsdp'=8,'tensor'=4] {'fsdp'}, dimensions={0}, use_global_device_ids=true | all-gather | bytes 995328 | tf_op jit(solution)/shard_map/all_gather | solution.py:102
  78.5 30.6 %all_gather.28 = bf16[2,3,64]{1,0,2:T(2,128)(2,1)S(1)} all-gather(bf16[2,3,8]{1,0,2:T(2,128)(2,1)S(1)} %copy.169), channel_id=1, replica_groups=mesh['fsdp'=8,'tensor'=4] {'fsdp'}, dimensions={2}, use_global_device_ids=true | all-gather | bytes 864 | tf_op jit(solution)/shard_map/all_gather | solution.py:106
  114.3 31.2 %all_gather.29 = bf16[192,768]{0,1:T(8,128)(2,1)S(1)} all-gather(bf16[192,96]{0,1:T(8,128)(2,1)S(1)} %copy.177), channel_id=1, replica_groups=mesh['fsdp'=8,'tensor'=4] {'fsdp'}, dimensions={1}, use_global_device_ids=true | all-gather | bytes 331776 | tf_op jit(solution)/shard_map/all_gather | solution.py:103
  147.7 26.1 %all_gather.31 = bf16[12,64]{0,1:T(8,128)(2,1)S(1)} all-gather(bf16[12,8]{0,1:T(8,128)(2,1)S(1)} %convert_element_type.125), channel_id=1, replica_groups=mesh['fsdp'=8,'tensor'=4] {'fsdp'}, dimensions={1}, use_global_device_ids=true | all-gather | bytes 1728 | tf_op jit(solution)/shard_map/all_gather | solution.py:107
  177.0 3.0 all-reduce.8.cloned.1.call-done
  183.1 7.6 %all-gather.4.cloned.1.call-done = bf16[768,768]{1,0:T(8,128)(2,1)} async-done(((bf16[96,768]{1,0:T(8,128)(2,1)}), bf16[768,768]{1,0:T(8,128)(2,1)}) %all-gather.4.cloned.1.call-update) | async-done | bytes 1179664 | tf_op jit(solution)/shard_map/all_gather | solution.py:104
  190.7 5.6 fusion.17
  199.6 68.5 %reduce-scatter.16.cloned.1.call-done = f32[768,96]{0,1:T(8,128)} async-done(((f32[768,768]{0,1:T(8,128)}), f32[768,96]{0,1:T(8,128)}) %reduce-scatter.16.cloned.1.call-update) | async-done | bytes 294928 | tf_op jit(solution)/shard_map/reduce_scatter | solution.py:207
  268.0 2.4 fusion.54
  270.7 40.6 %all-gather.6.cloned.1.call-done = bf16[768,768]{0,1:T(8,128)(2,1)} async-done(((bf16[768,96]{0,1:T(8,128)(2,1)}), bf16[768,768]{0,1:T(8,128)(2,1)}) %all-gather.6.cloned.1.call-update) | async-done | bytes 1179664 | tf_op jit(solution)/shard_map/all_gather | solution.py:105
  311.3 3.6 fusion.83
  317.3 3.0 convolution_convert_fusion.1
  320.3 29.3 %all-reduce.10.cloned.1.call-done = bf16[394,768]{1,0:T(8,128)(2,1)} async-done(((bf16[394,768]{1,0:T(8,128)(2,1)}), bf16[394,768]{1,0:T(8,128)(2,1)}) %all-reduce.10.cloned.1.call-update) | async-done | bytes 605200 | tf_op jit(solution)/shard_map/psum | solution.py:163
  349.6 2.4 fusion.22
  369.1 37.1 %all-reduce.12.cloned.1.call-done = (bf16[394,768]{1,0:T(8,128)(2,1)}, bf16[394,768]{1,0:T(8,128)(2,1)}) async-done(((bf16[394,768]{1,0:T(8,128)(2,1)}, bf16[394,768]{1,0:T(8,128)(2,1)}), (bf16[394,768]{1,0:T(8,128)(2,1)}, bf16[394,768]{1,0:T(8,128)(2,1)})) %all-reduce.12.cloned.1.call-update) | async-done | bytes 1210384 | tf_op jit(solution)/shard_map/psum | solution.py:135
  411.1 3.7 fusion.36
  415.9 2.4 fusion.40
  422.1 37.1 %all-reduce.2 = (f32[2,3,64]{2,0,1:T(2,128)S(1)}, f32[12,64]{1,0:T(8,128)S(1)}) all-reduce(f32[2,3,64]{2,0,1:T(2,128)S(1)} %pad_maximum_fusion.8, f32[12,64]{1,0:T(8,128)S(1)} %reshape.214), channel_id=6, replica_groups=mesh['fsdp'=8,'tensor'=4] {'fsdp'}, use_global_device_ids=true, to_apply=%region_21.0.clone | all-reduce | flops 1152 | bytes 9216
  461.9 2.7 fusion.9
  469.4 2.3 reduce-scatter.20.cloned.1.call-done
  473.9 63.7 %reduce-scatter.18.cloned.1.call-done = f32[96,192]{1,0:T(8,128)} async-done(((f32[768,192]{1,0:T(8,128)}), f32[96,192]{1,0:T(8,128)}) %reduce-scatter.18.cloned.1.call-update) | async-done | bytes 73744
  540.0 70.5 %reduce-scatter.12.cloned.1.call-done = f32[96,3,192]{2,0,1:T(8,128)} async-done(((f32[768,3,192]{2,0,1:T(8,128)}), f32[96,3,192]{2,0,1:T(8,128)}) %reduce-scatter.12.cloned.1.call-update) | async-done | bytes 221200 | tf_op jit(solution)/shard_map/reduce_scatter | solution.py:204
  613.3 70.1 %reduce-scatter.14.cloned.1.call-done = f32[96,768]{1,0:T(8,128)} async-done(((f32[768,768]{1,0:T(8,128)}), f32[96,768]{1,0:T(8,128)}) %reduce-scatter.14.cloned.1.call-update) | async-done | bytes 294928 | tf_op jit(solution)/shard_map/reduce_scatter | solution.py:206
  (300 shorter events, 69.6 us)
Async XLA Ops:
  8.0 172.0 %all-reduce.8.cloned.1.call-start = ((), (), s32[]{:S(2)}) async-start(), calls=%async_computation.5 | async-start | bytes 1228800 | tf_op jit(solution)/shard_map/psum | solution.py:126
  39.7 69.9 %copy-start.34 = (f32[768]{0:T(1024)}, f32[768]{0:T(1024)S(1)}, u32[]{:S(2)}) copy-start(f32[768]{0:T(1024)S(1)} %get-tuple-element.151) | copy-start | bytes 9220
  39.7 69.9 %copy-start.73 = (f32[768]{0:T(1024)}, f32[768]{0:T(1024)S(1)}, u32[]{:S(2)}) copy-start(f32[768]{0:T(1024)S(1)} %get-tuple-element.150) | copy-start | bytes 9220
  39.9 69.7 %copy-start.2 = (f32[394,768]{1,0:T(8,128)}, f32[394,768]{1,0:T(8,128)S(1)}, u32[]{:S(2)}) copy-start(f32[394,768]{1,0:T(8,128)S(1)} %reshape.207) | copy-start | bytes 3631108
  40.1 69.6 %copy-start.45 = (f32[394]{0:T(512)}, f32[394]{0:T(512)S(1)}, u32[]{:S(2)}) copy-start(f32[394]{0:T(512)S(1)} %rsqrt.20) | copy-start | bytes 4732
  40.7 68.9 %copy-start.48 = (f32[394]{0:T(512)}, f32[394]{0:T(512)S(1)}, u32[]{:S(2)}) copy-start(f32[394]{0:T(512)S(1)} %div.132) | copy-start | bytes 4732
  146.9 43.8 %all-gather.4.cloned.1.call-start = ((), (), s32[]{:S(2)}) async-start(), calls=%async_computation.6 | async-start | bytes 1327104 | tf_op jit(solution)/shard_map/all_gather | solution.py:104
  147.6 120.4 %reduce-scatter.16.cloned.1.call-start = ((), (), s32[]{:S(2)}) async-start(), calls=%async_computation.11 | async-start | bytes 2654208 | tf_op jit(solution)/shard_map/reduce_scatter | solution.py:207
  199.5 111.7 %all-gather.6.cloned.1.call-start = ((), (), s32[]{:S(2)}) async-start(), calls=%async_computation.7 | async-start | bytes 1327104 | tf_op jit(solution)/shard_map/all_gather | solution.py:105
  270.5 79.1 %all-reduce.10.cloned.1.call-start = ((), (), s32[]{:S(2)}) async-start(), calls=%async_computation.8 | async-start | bytes 1228800 | tf_op jit(solution)/shard_map/psum | solution.py:163
  317.2 89.0 %all-reduce.12.cloned.1.call-start = ((), (), s32[]{:S(2)}) async-start(), calls=%async_computation.14 | async-start | bytes 2457600 | tf_op jit(solution)/shard_map/psum | solution.py:135
  367.6 104.2 %reduce-scatter.20.cloned.1.call-start = ((), (), s32[]{:S(2)}) async-start(), calls=%async_computation.13 | async-start | bytes 442368
  409.5 128.0 %reduce-scatter.18.cloned.1.call-start = ((), (), s32[]{:S(2)}) async-start(), calls=%async_computation.12 | async-start | bytes 884736
  411.0 199.5 %reduce-scatter.12.cloned.1.call-start = ((), (), s32[]{:S(2)}) async-start(), calls=%async_computation.9 | async-start | bytes 2654208 | tf_op jit(solution)/shard_map/reduce_scatter | solution.py:204
  414.8 268.6 %reduce-scatter.14.cloned.1.call-start = ((), (), s32[]{:S(2)}) async-start(), calls=%async_computation.10 | async-start | bytes 2654208 | tf_op jit(solution)/shard_map/reduce_scatter | solution.py:206
  418.4 42.3 %copy-start.58 = (f32[12,8]{0,1:T(8,128)S(1)}, f32[12,8]{0,1:T(8,128)}, u32[]{:S(2)}) copy-start(f32[12,8]{0,1:T(8,128)} %param.25) | copy-start | bytes 1156
  418.4 43.5 %copy-start.6 = (bf16[394,768]{1,0:T(8,128)(2,1)S(1)}, bf16[394,768]{1,0:T(8,128)(2,1)}, u32[]{:S(2)}) copy-start(bf16[394,768]{1,0:T(8,128)(2,1)} %get-tuple-element.155) | copy-start | bytes 1815556
  468.0 70.5 %copy-start.31 = (f32[2,192,96]{2,1,0:T(8,128)S(1)}, f32[2,192,96]{2,1,0:T(8,128)}, u32[]{:S(2)}) copy-start(f32[2,192,96]{2,1,0:T(8,128)} %param.28) | copy-start | bytes 442372
  468.1 142.4 %copy-start.19 = (f32[96,3,192]{2,0,1:T(8,128)S(1)}, f32[96,3,192]{2,0,1:T(8,128)}, u32[]{:S(2)}) copy-start(f32[96,3,192]{2,0,1:T(8,128)} %param.20) | copy-start | bytes 663556
  468.1 142.4 %copy-start.25 = (f32[2,96,3,192]{3,1,2,0:T(8,128)S(1)}, f32[2,96,3,192]{3,1,2,0:T(8,128)}, u32[]{:S(2)}) copy-start(f32[2,96,3,192]{3,1,2,0:T(8,128)} %param.27) | copy-start | bytes 1327108
  472.6 139.8 %copy-start.61 = (f32[6,96]{1,0:T(8,128)}, f32[6,96]{1,0:T(8,128)S(1)}, u32[]{:S(2)}) copy-start(f32[6,96]{1,0:T(8,128)S(1)} %copy.209) | copy-start | bytes 6916
  538.5 73.9 %copy-start.28 = (f32[192,96]{1,0:T(8,128)}, f32[192,96]{1,0:T(8,128)S(1)}, u32[]{:S(2)}) copy-start(f32[192,96]{1,0:T(8,128)S(1)} %copy.203) | copy-start | bytes 221188
  540.0 143.4 %copy-start.21 = (f32[96,768]{1,0:T(8,128)S(1)}, f32[96,768]{1,0:T(8,128)}, u32[]{:S(2)}) copy-start(f32[96,768]{1,0:T(8,128)} %param.22) | copy-start | bytes 884740
  540.0 143.4 %copy-start.26 = (f32[2,96,768]{2,1,0:T(8,128)S(1)}, f32[2,96,768]{2,1,0:T(8,128)}, u32[]{:S(2)}) copy-start(f32[2,96,768]{2,1,0:T(8,128)} %param.29) | copy-start | bytes 1769476
  (68 other events, 485.3 us)
Sparse Core Ops, SparseCore 0:
  147.0 32.9 all-reduce.7
  317.3 32.1 all-reduce.9
  367.7 38.4 all-reduce.11
Sparse Core Ops, SparseCore 1:
  150.1 40.5 all-gather.3
  199.6 68.4 reduce-scatter.15
  270.7 40.5 all-gather.5
  409.5 62.2 reduce-scatter.19
  475.1 62.4 reduce-scatter.17
  541.6 68.8 reduce-scatter.11
  614.4 68.9 reduce-scatter.13
where the time goes:
time: 694 us; the launch traced here: 693 us
  waiting for transfers between devices  393 us (57%)
  blocking collectives  188 us (27%)
  matrix products  34 us (5%)
  local copies, waits for them, and re-layouts  31 us (4%)
  other arithmetic  29.6 us (4%)
  between operations  16.8 us (2%)
    reduce_scatter x1, waiting for transfers between devices, on_device(): lax.psum_scatter(grad_inward, 'fsdp', scatter_dimension=0, tiled=True)  70.5 us
    reduce_scatter x1, waiting for transfers between devices, on_device(): lax.psum_scatter(grad_widen, 'fsdp', scatter_dimension=0, tiled=True)  70.1 us
    reduce_scatter x1, waiting for transfers between devices, on_device(): lax.psum_scatter(grad_narrow, 'fsdp', scatter_dimension=1, tiled=True)  68.5 us
    unnamed x12, waiting for transfers between devices  66.1 us
    all_gather x1, waiting for transfers between devices, on_device(): lax.all_gather(w_fc2.astype(low), 'fsdp', axis=1, tiled=True)  40.6 us
    psum x1, waiting for transfers between devices, on_device(): mlp_total = lax.psum(mlp_term, 'tensor').astype(jnp.float32)  37.1 us
    unnamed x1, blocking collectives  37.1 us
    all_gather x1, blocking collectives, on_device(): lax.all_gather(w_qkv.astype(low), 'fsdp', axis=0, tiled=True)  35.5 us
  transfers between devices with their start and end apart: 10, of which 10 were waited for; matrix products, arithmetic and copies ran while one was open for 5% of the time, Pallas kernels for 0%

commit v1 on v0

--- a/solution.py
+++ b/solution.py
@@ -1,6 +1,10 @@
+import functools
+
 import jax
 import jax.numpy as jnp
 from jax import lax
+from jax.experimental import pallas as pl
+from jax.experimental.pallas import tpu as pltpu
 from jax.sharding import PartitionSpec as P
 
 HD = 64
@@ -76,7 +80,222 @@
     return (fresh, jnp.stack([first, second]))
 
 
+MESH_ID = pl.DeviceIdType.MESH
+
+
+def exchange(fsdp, tensor, tag, gathers=(), reduces=(), terms=()):
+    far_n, across_n = fsdp // 2, tensor // 2
+    n_g, n_r, n_t = len(gathers), len(reduces), len(terms)
+    low = jnp.bfloat16
+
+    def kernel(*refs):
+        refs = list(refs)
+
+        def take(count):
+            out, refs[:] = refs[:count], refs[count:]
+            return out
+
+        g_in, r_in, t_in = take(n_g), take(n_r), take(n_t)
+        g_out, r_out, t_out = take(n_g), take(n_r), take(n_t)
+        r_near, r_sum, r_far = take(n_r), take(n_r), take(n_r)
+        t_core, t_half, t_across = take(n_t), take(n_t), take(n_t)
+        g_send, g_recv, r_send, r_recv, t_send, t_recv = take(6)
+        mine = lax.axis_index("fsdp")
+        lane = lax.axis_index("tensor")
+        far, near = lax.div(mine, 2), lax.rem(mine, 2)
+        across, core = lax.div(lane, 2), lax.rem(lane, 2)
+        twin = 2 * far + (1 - near)
+        mate = 2 * across + (1 - core)
+
+        def ahead(step):
+            return lax.rem(far + step, far_n)
+
+        def behind(step):
+            return lax.rem(far + far_n - step, far_n)
+
+        barrier = pltpu.get_barrier_semaphore()
+        greeted = 0
+        if n_g or n_r:
+            for who in [twin] + [2 * ahead(j) + near for j in range(1, far_n)]:
+                pl.semaphore_signal(barrier, inc=1, device_id=(who, lane), device_id_type=MESH_ID)
+                greeted += 1
+        if n_t:
+            for who in [mate] + [
+                2 * lax.rem(across + j, across_n) + core for j in range(1, across_n)
+            ]:
+                pl.semaphore_signal(barrier, inc=1, device_id=(mine, who), device_id_type=MESH_ID)
+                greeted += 1
+        pl.semaphore_wait(barrier, greeted)
+
+        def copy(src, dst, send, recv, target):
+            return pltpu.make_async_remote_copy(
+                src_ref=src,
+                dst_ref=dst,
+                send_sem=send,
+                recv_sem=recv,
+                device_id=target,
+                device_id_type=MESH_ID,
+            )
+
+        def run_gather():
+            sent = []
+            for j in range(1, far_n):
+                for p in range(n_g):
+                    sent.append(
+                        copy(g_in[p], g_out[p].at[mine], g_send.at[p, j], g_recv.at[p, j],
+                             (2 * ahead(j) + near, lane))
+                    )
+                    sent[-1].start()
+            for p in range(n_g):
+                sent.append(
+                    copy(g_in[p], g_out[p].at[mine], g_send.at[p, far_n], g_recv.at[p, far_n],
+                         (twin, lane))
+                )
+                sent[-1].start()
+                g_out[p][mine] = g_in[p][...]
+            yield
+            for j in range(1, far_n):
+                for p in range(n_g):
+                    slot = g_out[p].at[2 * behind(j) + near]
+                    copy(g_in[p], slot, g_send.at[p, j], g_recv.at[p, j],
+                         (2 * ahead(j) + near, lane)).wait_recv()
+                    sent.append(
+                        copy(slot, slot, g_send.at[p, far_n + j], g_recv.at[p, far_n + j],
+                             (twin, lane))
+                    )
+                    sent[-1].start()
+                yield
+            for j in range(far_n):
+                for p in range(n_g):
+                    slot = g_out[p].at[2 * behind(j) + (1 - near)]
+                    copy(g_in[p], slot, g_send.at[p, far_n + j], g_recv.at[p, far_n + j],
+                         (twin, lane)).wait_recv()
+            for entry in sent:
+                entry.wait_send()
+
+        def run_reduce():
+            order = list(range(1, far_n)) + [0]
+            hops = {}
+            for p in range(n_r):
+                for j in order:
+                    hops[p, j] = copy(
+                        r_in[p].at[2 * ahead(j) + (1 - near)], r_near[p].at[j],
+                        r_send.at[p, j], r_recv.at[p, j], (twin, lane))
+                    hops[p, j].start()
+            yield
+            sent = {}
+            for p in range(n_r):
+                for j in range(1, far_n):
+                    hops[p, j].wait_recv()
+                    total = r_in[p][2 * ahead(j) + near].astype(jnp.float32) + r_near[p][j].astype(
+                        jnp.float32
+                    )
+                    r_sum[p][j - 1] = total.astype(r_sum[p].dtype)
+                    sent[p, j] = copy(
+                        r_sum[p].at[j - 1], r_far[p].at[j - 1],
+                        r_send.at[p, far_n + j], r_recv.at[p, far_n + j],
+                        (2 * ahead(j) + near, lane))
+                    sent[p, j].start()
+                    yield
+            for p in range(n_r):
+                hops[p, 0].wait_recv()
+                total = r_in[p][mine].astype(jnp.float32) + r_near[p][0].astype(jnp.float32)
+                for j in range(1, far_n):
+                    sent[p, j].wait_recv()
+                    total = total + r_far[p][j - 1].astype(jnp.float32)
+                r_out[p][...] = total
+            for entry in list(hops.values()) + list(sent.values()):
+                entry.wait_send()
+
+        def run_terms():
+            half = [ref.shape[1] // 2 for ref in t_in]
+            own = [pl.ds(pl.multiple_of(core * h, h), h) for h in half]
+            other = [pl.ds(pl.multiple_of((1 - core) * h, h), h) for h in half]
+            first, second, third = {}, {}, {}
+            for p in range(n_t):
+                first[p] = copy(t_in[p].at[:, other[p]], t_core[p], t_send.at[p, 0],
+                                t_recv.at[p, 0], (mine, mate))
+                first[p].start()
+            yield
+            for p in range(n_t):
+                first[p].wait_recv()
+                t_half[p][...] = (
+                    t_in[p][:, own[p]].astype(jnp.float32) + t_core[p][...].astype(jnp.float32)
+                ).astype(low)
+                for j in range(1, across_n):
+                    second[p, j] = copy(
+                        t_half[p], t_across[p].at[j - 1], t_send.at[p, 1 + j], t_recv.at[p, 1 + j],
+                        (mine, 2 * lax.rem(across + j, across_n) + core))
+                    second[p, j].start()
+            yield
+            yield
+            for p in range(n_t):
+                total = t_half[p][...].astype(jnp.float32)
+                for j in range(1, across_n):
+                    second[p, j].wait_recv()
+                    total = total + t_across[p][j - 1].astype(jnp.float32)
+                t_out[p][:, own[p]] = total.astype(low)
+                third[p] = copy(t_out[p].at[:, own[p]], t_out[p].at[:, own[p]], t_send.at[p, 1],
+                                t_recv.at[p, 1], (mine, mate))
+                third[p].start()
+            yield
+            for p in range(n_t):
+                copy(t_out[p].at[:, own[p]], t_out[p].at[:, other[p]], t_send.at[p, 1],
+                     t_recv.at[p, 1], (mine, mate)).wait_recv()
+            for entry in list(first.values()) + list(second.values()) + list(third.values()):
+                entry.wait_send()
+
+        flows = []
+        if n_t:
+            flows.append(run_terms())
+        if n_g:
+            flows.append(run_gather())
+        if n_r:
+            flows.append(run_reduce())
+        while flows:
+            for flow in list(flows):
+                if next(flow, "end") == "end":
+                    flows.remove(flow)
+
+    shape = jax.ShapeDtypeStruct
+    outs = (
+        [shape((fsdp,) + a.shape, a.dtype) for a in gathers]
+        + [shape(a.shape[1:], jnp.float32) for a in reduces]
+        + [shape(a.shape, a.dtype) for a in terms]
+    )
+    few = max(far_n - 1, 1)
+    scratch = (
+        [pltpu.VMEM((far_n,) + a.shape[1:], a.dtype) for a in reduces]
+        + [pltpu.VMEM((few,) + a.shape[1:], a.dtype) for a in reduces]
+        + [pltpu.VMEM((few,) + a.shape[1:], a.dtype) for a in reduces]
+        + [pltpu.VMEM((a.shape[0], a.shape[1] // 2), low) for a in terms]
+        + [pltpu.VMEM((a.shape[0], a.shape[1] // 2), low) for a in terms]
+        + [pltpu.VMEM((max(across_n - 1, 1), a.shape[0], a.shape[1] // 2), low) for a in terms]
+        + [pltpu.SemaphoreType.DMA((max(n_g, 1), 2 * far_n))] * 2
+        + [pltpu.SemaphoreType.DMA((max(n_r, 1), 2 * far_n))] * 2
+        + [pltpu.SemaphoreType.DMA((max(n_t, 1), 1 + across_n))] * 2
+    )
+    args = tuple(gathers) + tuple(reduces) + tuple(terms)
+    return pl.pallas_call(
+        kernel,
+        out_shape=tuple(outs),
+        in_specs=[pl.BlockSpec(memory_space=pltpu.VMEM)] * len(args),
+        out_specs=tuple([pl.BlockSpec(memory_space=pltpu.VMEM)] * len(outs)),
+        scratch_shapes=scratch,
+        compiler_params=pltpu.CompilerParams(
+            collective_id=tag, has_side_effects=True, vmem_limit_bytes=48 * 1024 * 1024
+        ),
+        name="exchange_" + str(tag),
+    )(*args)
+
+
+def row_of(values, lanes):
+    return jnp.pad(values, [(0, 0)] * (values.ndim - 1) + [(0, lanes - values.shape[-1])])
+
+
 def on_device(
+    fsdp,
+    tensor,
     block_input,
     output_grad,
     live_images,
@@ -98,95 +317,146 @@
     low = jnp.bfloat16
     images, seqlen, width = block_input.shape
     rows = images * seqlen
-    inward, outward, widen, narrow, heads_bias, hidden_bias, norm_rows = (
-        lax.all_gather(w_qkv.astype(low), "fsdp", axis=0, tiled=True),
-        lax.all_gather(w_out.astype(low), "fsdp", axis=1, tiled=True),
-        lax.all_gather(w_fc1.astype(low), "fsdp", axis=0, tiled=True),
-        lax.all_gather(w_fc2.astype(low), "fsdp", axis=1, tiled=True),
-        lax.all_gather(qv_bias.astype(low), "fsdp", axis=2, tiled=True),
-        lax.all_gather(fc1_bias.astype(low), "fsdp", axis=1, tiled=True),
-        lax.all_gather(norm_vec.astype(low), "fsdp", axis=1, tiled=True),
-    )
-    local_feat = inward.shape[2]
+    owned_rows, _, local_feat = w_qkv.shape
+    hidden = w_fc1.shape[1]
     heads_here = local_feat // HD
-    vecf = norm_rows.astype(jnp.float32)
+    n_qvb, n_fc1b = qv_bias.size, fc1_bias.size
+    vec_rows = norm_vec.shape[0]
+    lanes = -(-max(owned_rows, n_qvb, n_fc1b) // 128) * 128
+    small_rows = 16
+
+    small = jnp.concatenate(
+        [
+            row_of(norm_vec, lanes),
+            row_of(fc1_bias.reshape(1, n_fc1b), lanes),
+            row_of(qv_bias.reshape(1, n_qvb), lanes),
+            jnp.zeros((small_rows - vec_rows - 2, lanes), jnp.float32),
+        ]
+    ).astype(low)
+    small_all, inward, outward = exchange(
+        fsdp,
+        tensor,
+        1,
+        gathers=(
+            small,
+            w_qkv.astype(low).reshape(owned_rows, 3 * local_feat),
+            w_out.astype(low).T,
+        ),
+    )
+    inward = inward.reshape(width, 3 * local_feat)
+    outward = outward.reshape(width, local_feat)
+    smallf = small_all.astype(jnp.float32)
+    vecf = smallf[:, :vec_rows, :owned_rows].transpose(1, 0, 2).reshape(vec_rows, width)
+    hidden_bias = (
+        smallf[:, vec_rows, :n_fc1b]
+        .reshape((fsdp,) + fc1_bias.shape)
+        .transpose(1, 0, 2)
+        .reshape(hidden)
+    )
+    biasf = (
+        smallf[:, vec_rows + 1, :n_qvb]
+        .reshape((fsdp,) + qv_bias.shape)
+        .transpose(1, 2, 0, 3)
+        .reshape(2, local_feat)
+    )
     flat = block_input.astype(jnp.float32).reshape(rows, width)
     first_norm, unit_one, scale_one = norm_forward(flat, vecf[0], vecf[1])
     normed_one = first_norm.astype(low)
-    projected = jnp.einsum("nd,dcj->ncj", normed_one, inward, preferred_element_type=jnp.float32)
-    biasf = heads_bias.astype(jnp.float32).reshape(2, local_feat)
-    shifts = jnp.stack([biasf[0], jnp.zeros_like(biasf[0]), biasf[1]])
-    triple = (projected + shifts).astype(low).reshape(images, seqlen, 3, heads_here, HD)
+    shifts = jnp.concatenate([biasf[0], jnp.zeros_like(biasf[0]), biasf[1]])
+    projected = jnp.dot(normed_one, inward, preferred_element_type=jnp.float32) + shifts
+    triple = projected.astype(low).reshape(images, seqlen, 3, heads_here, HD)
     queries = triple[:, :, 0]
     key_rows = triple[:, :, 1]
     value_rows = triple[:, :, 2]
     mixed, logsum = attend(queries, key_rows, value_rows)
     attn_rows = mixed.reshape(rows, local_feat)
-    attn_term = jnp.dot(attn_rows, outward, preferred_element_type=jnp.float32).astype(low)
-    attn_total = lax.psum(attn_term, "tensor").astype(jnp.float32)
-    resid = flat + attn_total + vecf[4]
+    attn_term = jnp.einsum(
+        "nj,dj->nd", attn_rows, outward, preferred_element_type=jnp.float32
+    ).astype(low)
+    widen, narrow, attn_total = exchange(
+        fsdp,
+        tensor,
+        2,
+        gathers=(w_fc1.astype(low), w_fc2.astype(low).T),
+        terms=(attn_term,),
+    )
+    widen = widen.reshape(width, hidden)
+    narrow = narrow.reshape(width, hidden)
+    resid = flat + attn_total.astype(jnp.float32) + vecf[4]
     second_norm, unit_two, scale_two = norm_forward(resid, vecf[2], vecf[3])
     normed_two = second_norm.astype(low)
-    pre_act = jnp.dot(normed_two, widen, preferred_element_type=jnp.float32) + hidden_bias.astype(
-        jnp.float32
-    ).reshape(-1)
+    pre_act = jnp.dot(normed_two, widen, preferred_element_type=jnp.float32) + hidden_bias
     activ = jax.nn.gelu(pre_act, approximate=False).astype(low)
-    mlp_term = jnp.dot(activ, narrow, preferred_element_type=jnp.float32).astype(low)
-    mlp_total = lax.psum(mlp_term, "tensor").astype(jnp.float32)
+    mlp_term = jnp.einsum(
+        "nf,df->nd", activ, narrow, preferred_element_type=jnp.float32
+    ).astype(low)
     row_mask = jnp.broadcast_to(live_images.astype(jnp.float32)[:, None], (images, seqlen)).reshape(
         rows, 1
     )
-    block_output = (
-        (row_mask * (resid + mlp_total + vecf[5])).astype(low).reshape(images, seqlen, width)
-    )
-    inward, outward, widen, narrow, norm_rows = (
-        lax.all_gather(w_qkv.astype(low), "fsdp", axis=0, tiled=True),
-        lax.all_gather(w_out.astype(low), "fsdp", axis=1, tiled=True),
-        lax.all_gather(w_fc1.astype(low), "fsdp", axis=0, tiled=True),
-        lax.all_gather(w_fc2.astype(low), "fsdp", axis=1, tiled=True),
-        lax.all_gather(norm_vec.astype(low), "fsdp", axis=1, tiled=True),
-    )
-    vecf = norm_rows.astype(jnp.float32)
     grad_flat = output_grad.astype(jnp.float32).reshape(rows, width) * row_mask
     grad_low = grad_flat.astype(low)
-    grad_narrow = jnp.einsum("nf,nd->fd", activ, grad_low, preferred_element_type=jnp.float32)
-    delta_act = jnp.einsum("nd,fd->nf", grad_low, narrow, preferred_element_type=jnp.float32)
+    grad_narrow = jnp.einsum("nd,nf->df", grad_low, activ, preferred_element_type=jnp.float32)
+    delta_act = jnp.einsum("nd,df->nf", grad_low, narrow, preferred_element_type=jnp.float32)
     delta_pre = delta_act * gelu_slope(pre_act)
     delta_pre_low = delta_pre.astype(low)
-    grad_hidden = jnp.sum(delta_pre, axis=0).reshape(hidden_bias.shape)
+    grad_hidden = jnp.sum(delta_pre, axis=0)
     grad_widen = jnp.einsum(
         "nd,nf->df", normed_two, delta_pre_low, preferred_element_type=jnp.float32
     )
     two_term = jnp.einsum(
         "nf,df->nd", delta_pre_low, widen, preferred_element_type=jnp.float32
     ).astype(low)
-    delta_two = lax.psum(two_term, "tensor").astype(jnp.float32)
+
+    def blocks(grad):
+        return grad.astype(low).reshape(fsdp, owned_rows, grad.shape[1])
+
+    own_narrow, own_widen, delta_two, mlp_total = exchange(
+        fsdp,
+        tensor,
+        3,
+        reduces=(blocks(grad_narrow), blocks(grad_widen)),
+        terms=(two_term, mlp_term),
+    )
+    delta_two = delta_two.astype(jnp.float32)
+    block_output = (
+        (row_mask * (resid + mlp_total.astype(jnp.float32) + vecf[5]))
+        .astype(low)
+        .reshape(images, seqlen, width)
+    )
     delta_resid = grad_flat + norm_backward(delta_two, unit_two, scale_two, vecf[2])
     delta_resid_low = delta_resid.astype(low)
     grad_outward = jnp.einsum(
-        "nj,nd->jd", attn_rows, delta_resid_low, preferred_element_type=jnp.float32
-    )
-    delta_mixed = jnp.einsum(
-        "nd,jd->nj", delta_resid_low, outward, preferred_element_type=jnp.float32
-    )
+        "nd,nj->dj", delta_resid_low, attn_rows, preferred_element_type=jnp.float32
+    )
+    delta_mixed = jnp.dot(delta_resid_low, outward, preferred_element_type=jnp.float32)
     delta_mixed = delta_mixed.astype(low).reshape(images, seqlen, heads_here, HD)
     delta_query, delta_key, delta_value = attend_back(
         queries, key_rows, value_rows, logsum, delta_mixed
     )
     delta_triple = jnp.stack([delta_query, delta_key, delta_value], axis=2).reshape(
-        rows, 3, local_feat
+        rows, 3 * local_feat
     )
     grad_heads = jnp.stack(
-        [jnp.sum(delta_triple[:, 0], axis=0), jnp.sum(delta_triple[:, 2], axis=0)]
-    ).reshape(2, heads_here, HD)
+        [
+            jnp.sum(delta_query, axis=(0, 1)).reshape(local_feat),
+            jnp.sum(delta_value, axis=(0, 1)).reshape(local_feat),
+        ]
+    )
     triple_low = delta_triple.astype(low)
     grad_inward = jnp.einsum(
-        "nd,ncj->dcj", normed_one, triple_low, preferred_element_type=jnp.float32
+        "nd,nj->dj", normed_one, triple_low, preferred_element_type=jnp.float32
     )
     one_term = jnp.einsum(
-        "ncj,dcj->nd", triple_low, inward, preferred_element_type=jnp.float32
+        "nj,dj->nd", triple_low, inward, preferred_element_type=jnp.float32
     ).astype(low)
-    delta_one = lax.psum(one_term, "tensor").astype(jnp.float32)
+    own_inward, own_outward, delta_one = exchange(
+        fsdp,
+        tensor,
+        4,
+        reduces=(blocks(grad_inward), blocks(grad_outward)),
+        terms=(one_term,),
+    )
+    delta_one = delta_one.astype(jnp.float32)
     input_grad = (delta_resid + norm_backward(delta_one, unit_one, scale_one, vecf[0])).reshape(
         images, seqlen, width
     )
@@ -200,14 +470,35 @@
             jnp.sum(grad_flat, axis=0),
         ]
     )
+    r_fc1b, c_fc1b = fc1_bias.shape
+    k_qvb, r_qvb, c_qvb = qv_bias.shape
+    small_grads = jnp.concatenate(
+        [
+            row_of(grad_rows_vec.reshape(vec_rows, fsdp, owned_rows).transpose(1, 0, 2), lanes),
+            row_of(
+                grad_hidden.reshape(r_fc1b, fsdp, c_fc1b).transpose(1, 0, 2).reshape(
+                    fsdp, 1, n_fc1b
+                ),
+                lanes,
+            ),
+            row_of(
+                grad_heads.reshape(k_qvb, r_qvb, fsdp, c_qvb).transpose(2, 0, 1, 3).reshape(
+                    fsdp, 1, n_qvb
+                ),
+                lanes,
+            ),
+        ],
+        axis=1,
+    )
+    (own_small,) = exchange(fsdp, tensor, 5, reduces=(small_grads,))
     owned = (
-        lax.psum_scatter(grad_inward, "fsdp", scatter_dimension=0, tiled=True),
-        lax.psum_scatter(grad_outward, "fsdp", scatter_dimension=1, tiled=True),
-        lax.psum_scatter(grad_widen, "fsdp", scatter_dimension=0, tiled=True),
-        lax.psum_scatter(grad_narrow, "fsdp", scatter_dimension=1, tiled=True),
-        lax.psum_scatter(grad_heads, "fsdp", scatter_dimension=2, tiled=True),
-        lax.psum_scatter(grad_hidden, "fsdp", scatter_dimension=1, tiled=True),
-        lax.psum_scatter(grad_rows_vec, "fsdp", scatter_dimension=1, tiled=True),
+        own_inward.reshape(w_qkv.shape),
+        own_outward.T,
+        own_widen,
+        own_narrow.T,
+        own_small[vec_rows + 1, :n_qvb].reshape(qv_bias.shape),
+        own_small[vec_rows, :n_fc1b].reshape(fc1_bias.shape),
+        own_small[:vec_rows, :owned_rows],
     )
     params = (w_qkv, w_out, w_fc1, w_fc2, qv_bias, fc1_bias, norm_vec)
     moments = (mom_qkv, mom_out, mom_fc1, mom_fc2, mom_qvb, mom_fc1b, mom_vec)
@@ -222,7 +513,7 @@
 
 def solution(mesh):
     return jax.shard_map(
-        on_device,
+        functools.partial(on_device, mesh.shape["fsdp"], mesh.shape["tensor"]),
         mesh=mesh,
         in_specs=(
             P("fsdp", None, None),

time: 694 us -> 234 us (0.34)
  waiting for transfers between devices: 393 us -> 0 us
  blocking collectives: 188 us -> 0 us
  Pallas kernels: 0 us -> 136 us
  between operations: 16.8 us -> 1.72 us
  local copies, waits for them, and re-layouts: 31 us -> 45 us
    reduce_scatter x3 -> x0, waiting for transfers between devices: 209 us -> none  [the longest x1 70.5 us: on_device(): lax.psum_scatter(grad_inward, 'fsdp', scatter_dimension=0, tiled=True)]
    all_gather x5 -> x0, blocking collectives: 151 us -> none  [the longest x1 35.5 us: on_device(): lax.all_gather(w_qkv.astype(low), 'fsdp', axis=0, tiled=True)]
    pallas_call x0 -> x5, Pallas kernels: none -> 136 us  [exchange(): pl.pallas_call(kernel, out_shape=tuple(outs), in_specs=[pl.BlockSpec(memo...]
    psum x3 -> x0, waiting for transfers between devices: 69.4 us -> none  [the longest x1 37.1 us: on_device(): mlp_total = lax.psum(mlp_term, 'tensor').astype(jnp.float32)]
    unnamed x12 -> x0, waiting for transfers between devices: 66.1 us -> none
    all_gather x2 -> x0, waiting for transfers between devices: 48.1 us -> none  [the longest x1 40.6 us: on_device(): lax.all_gather(w_fc2.astype(low), 'fsdp', axis=1, tiled=True)]
    unnamed x1 -> x0, blocking collectives: 37.1 us -> none
    another operation x15 -> x12, other arithmetic: 14.3 us -> 5.07 us  [adamw(): return (fresh, jnp.stack([first, second]))]
  transfers between devices with their start and end apart: 10 -> 0, of which waited for: 10 -> 0; matrix products, arithmetic and copies ran while one was open for 5% -> 0% of each run, Pallas kernels for 0% -> 0%
where the time goes in v1:
time: 234 us; the launch traced here: 233 us
  Pallas kernels  136 us (58%)
  local copies, waits for them, and re-layouts  45 us (19%)
  matrix products  27.4 us (12%)
  other arithmetic  23 us (10%)
    pallas_call x5, Pallas kernels, exchange(): pl.pallas_call(kernel, out_shape=tuple(outs), in_specs=[pl.BlockSpec(memo...  136 us
    unnamed x136, local copies, waits for them, and re-layouts  22.9 us
    dot_general x1, matrix products, on_device(): jnp.dot(normed_two, widen, preferred_element_type=jnp.float32) + hidden_bias  5.56 us
    another operation x12, other arithmetic, adamw(): return (fresh, jnp.stack([first, second]))  5.07 us

profile of v1, /device:TPU:0, one launch (start us, length us, event | category | flops | bytes accessed | tf_op | source)
XLA Modules:
  0.0 232.8 jit_solution(6414826665010993136)
XLA Ops:
  3.6 26.8 %exchange_1.1 = (bf16[8,16,128]{2,1,0:T(8,128)(2,1)S(1)}, bf16[8,96,576]{2,1,0:T(8,128)(2,1)S(1)}, bf16[8,96,192]{2,1,0:T(8,128)(2,1)S(1)}) custom-call(bf16[16,128]{1,0:T(8,128)(2,1)S(1)} %fusion.94.refs_0_, bf16[96,576]{1,0:T(8,128)(2,1)S(1)} %copy.251.refs_1_, bf16[96,192]{1,0:T(8,128)(2,1)S(1)} %convert_bitcast_fusion.3.refs_2_), custom_call_target="tpu_custom_call" | custom-call | tf_op jit(solution)/shard_map/exchange_1/pallas_call | solution.py:279
  33.2 1.4 add_convert_fusion.1
  36.0 1.7 fusion.6
  45.5 33.9 %exchange_2.1 = (bf16[8,96,768]{2,1,0:T(8,128)(2,1)S(1)}, bf16[8,96,768]{2,1,0:T(8,128)(2,1)S(1)}, bf16[394,768]{1,0:T(8,128)(2,1)S(1)}) custom-call(bf16[96,768]{1,0:T(8,128)(2,1)S(1)} %convert_element_type.138.refs_0_, bf16[96,768]{1,0:T(8,128)(2,1)S(1)} %convert_bitcast_fusion.2.refs_1_, bf16[394,768]{1,0:T(8,128)(2,1)S(1)} %convolution_convert_fusion.6.refs_2_), custom_call_target="tpu_custom_call" | custom-call | tf_op jit(solution)/shard_map/exchange_2/pallas_call | solution.py:279
  81.7 1.4 reshape.414
  85.9 5.6 %fusion.17 = (bf16[394,768]{1,0:T(8,128)(2,1)S(1)}, f32[394,768]{1,0:T(8,128)}) fusion(f32[768]{0:T(1024)S(1)} %add.254, bf16[768,768]{1,0:T(8,128)(2,1)S(1)} %bitcast.211, f32[394,768]{1,0:T(8,128)} %copy-done.12, f32[768]{0:T(1024)S(1)} %add.251, f32[768]{0:T(1024)S(1)} %mul.612, f32[394]{0:T(512)S(1)} %add_rsqrt_fusion.1, ...), kind=kOutput, calls=%fused_computation.36 | convolution fusion | flops 486265344 | bytes 4217936 | tf_op jit(solution)/shard_map/dot_general | solution.py:388
  94.8 2.7 %fusion.115 = (f32[768]{0:T(1024)S(1)}, bf16[394,768]{1,0:T(8,128)(2,1)S(1)}) fusion(f32[394,768]{1,0:T(8,128)} %get-tuple-element.205, bf16[394,768]{1,0:T(8,128)(2,1)} %convert_element_type.157, bf16[768,768]{1,0:T(8,128)(2,1)} %bitcast.213), kind=kOutput, calls=%fused_computation.241 | convolution fusion | flops 468109056 | bytes 3603456 | tf_op jit(solution)/shard_map/nd,df->nf/dot_general | solution.py:399
  97.5 1.5 convolution_convert_fusion.5.refs_2_
  101.6 2.5 %reshape.422 = f32[394,768]{1,0:T(8,128)} reshape(f32[2,197,768]{2,1,0:T(8,128)} %copy.261) | data formatting | bytes 2420736 | tf_op jit(solution)/shard_map/reshape | solution.py:396
  104.1 2.2 convolution_convert_fusion.1
  106.4 40.0 %exchange_3.1 = (f32[96,768]{1,0:T(8,128)S(1)}, f32[96,768]{1,0:T(8,128)S(1)}, bf16[394,768]{1,0:T(8,128)(2,1)S(1)}, bf16[394,768]{1,0:T(8,128)(2,1)S(1)}) custom-call(bf16[8,96,768]{2,1,0:T(8,128)(2,1)S(1)} %bitcast.208, bf16[8,96,768]{2,1,0:T(8,128)(2,1)S(1)} %bitcast.207, bf16[394,768]{1,0:T(8,128)(2,1)S(1)} %copy-done, ...), custom_call_target="tpu_custom_call" | custom-call | tf_op jit(solution)/shard_map/exchange_3/pallas_call | solution.py:279
  148.3 3.6 %fusion.103 = (f32[768]{0:T(1024)S(1)}, f32[394,768]{1,0:T(8,128)}, bf16[394,768]{1,0:T(8,128)(2,1)}) fusion(f32[394]{0:T(512)S(1)} %broadcast_multiply_fusion.3, f32[394,768]{1,0:T(8,128)} %copy-done.12, f32[394]{0:T(512)S(1)} %broadcast_multiply_fusion.5, f32[394]{0:T(512)S(1)} %broadcast_multiply_fusion.4, f32[768]{0:T(1024)S(1)} %mul.612, ...), kind=kLoop, calls=%fused_computation.230 | loop fusion | flops 4840704 | bytes 5463752 | tf_op jit(solution)/shard_map/reduce_sum | solution.py:469
  151.9 1.7 convolution_convert_fusion.9
  153.8 1.8 multiply_reduce_fusion
  159.5 1.9 convolution_convert_fusion.3.refs_2_
  161.3 1.7 convolution_convert_fusion.7
  163.2 2.6 %convolution_convert_fusion.2 = bf16[768,576]{0,1:T(8,128)(2,1)} fusion(bf16[394,768]{1,0:T(8,128)(2,1)S(1)} %copy-done.34, bf16[394,576]{0,1:T(8,128)(2,1)} %convert_element_type.168), kind=kOutput, calls=%fused_computation.16 | convolution fusion | flops 349028352 | bytes 1943808 | tf_op jit(solution)/shard_map/nd,nj->dj/dot_general | solution.py:446
  165.8 1.8 copy.270
  167.6 26.1 %exchange_4.1 = (f32[96,576]{1,0:T(8,128)S(1)}, f32[96,192]{1,0:T(8,128)S(1)}, bf16[394,768]{1,0:T(8,128)(2,1)S(1)}) custom-call(bf16[8,96,576]{2,1,0:T(8,128)(2,1)S(1)} %bitcast.203, bf16[8,96,192]{2,1,0:T(8,128)(2,1)S(1)} %bitcast.206, bf16[394,768]{1,0:T(8,128)(2,1)S(1)} %convolution_convert_fusion.3.refs_2_), custom_call_target="tpu_custom_call" | custom-call | tf_op jit(solution)/shard_map/exchange_4/pallas_call | solution.py:279
  195.7 2.0 fusion.23
  198.7 8.9 %exchange_5.1 = f32[8,128]{1,0:T(8,128)S(1)} custom-call(f32[8,8,128]{2,1,0:T(8,128)S(1)} %select_maximum_fusion.refs_0_), custom_call_target="tpu_custom_call" | custom-call | tf_op jit(solution)/shard_map/exchange_5/pallas_call | solution.py:279
  220.2 3.1 %fusion.9 = f32[394,768]{1,0:T(8,128)} fusion(f32[394,768]{1,0:T(8,128)} %get-tuple-element.158, bf16[394,768]{1,0:T(8,128)(2,1)S(1)} %get-tuple-element.44, f32[394,768]{1,0:T(8,128)} %copy-done.11, f32[394]{0:T(512)S(1)} %broadcast_multiply_fusion.1, f32[394]{0:T(512)S(1)} %div.138, f32[394]{0:T(512)S(1)} %broadcast_multiply_fusion.2, f32[768]{0:T(1024)S(1)} %mul.604, ...), kind=kLoop, calls=%fused_computation.28 | loop fusion | flops 2723328 | bytes 4245664 | tf_op jit(solution)/shard_map/add | solution.py:460
  223.3 1.4 reshape.431
  224.7 1.6 copy.303
  (266 shorter events, 53.1 us)
Async XLA Ops:
  0.7 2.5 %copy-start.41 = (f32[12,8]{0,1:T(8,128)S(1)}, f32[12,8]{0,1:T(8,128)}, u32[]{:S(2)}) copy-start(f32[12,8]{0,1:T(8,128)} %param.25) | copy-start | bytes 1156
  0.7 2.7 %copy-start.46 = (f32[2,3,8]{2,0,1:T(2,128)S(1)}, f32[2,3,8]{2,0,1:T(2,128)}, u32[]{:S(2)}) copy-start(f32[2,3,8]{2,0,1:T(2,128)} %param.24) | copy-start | bytes 580
  0.7 2.8 %copy-start.43 = (f32[6,96]{1,0:T(8,128)S(1)}, f32[6,96]{1,0:T(8,128)}, u32[]{:S(2)}) copy-start(f32[6,96]{1,0:T(8,128)} %param.26) | copy-start | bytes 6916
  0.7 30.7 %copy-start.15 = (bf16[2,197,768]{2,0,1:T(2,128)(2,1)S(1)}, bf16[2,197,768]{2,0,1:T(2,128)(2,1)}, u32[]{:S(2)}) copy-start(bf16[2,197,768]{2,0,1:T(2,128)(2,1)} %param.17) | copy-start | bytes 1815556
  30.4 5.6 %copy-start.7 = (bf16[8,96,576]{2,1,0:T(8,128)(2,1)}, bf16[8,96,576]{2,1,0:T(8,128)(2,1)S(1)}, u32[]{:S(2)}) copy-start(bf16[8,96,576]{2,1,0:T(8,128)(2,1)S(1)} %get-tuple-element.37) | copy-start | bytes 2654212
  30.5 5.2 %copy-start.38 = (f32[8,16,128]{2,1,0:T(8,128)}, f32[8,16,128]{2,1,0:T(8,128)S(1)}, u32[]{:S(2)}) copy-start(f32[8,16,128]{2,1,0:T(8,128)S(1)} %convert_element_type.142) | copy-start | bytes 196612
  40.9 1.9 copy-start.25
  42.6 1.9 copy-start.9
  83.1 8.4 %copy-start.11 = (f32[394,768]{1,0:T(8,128)}, f32[394,768]{1,0:T(8,128)S(1)}, u32[]{:S(2)}) copy-start(f32[394,768]{1,0:T(8,128)S(1)} %reshape.414) | copy-start | bytes 3631108
  84.9 6.6 %copy-start.50 = (f32[768]{0:T(1024)}, f32[768]{0:T(1024)S(1)}, u32[]{:S(2)}) copy-start(f32[768]{0:T(1024)S(1)} %add.251) | copy-start | bytes 9220
  85.9 5.6 %copy-start.6 = (bf16[8,96,768]{2,1,0:T(8,128)(2,1)S(1)}, bf16[8,96,768]{2,1,0:T(8,128)(2,1)}, u32[]{:S(2)}) copy-start(bf16[8,96,768]{2,1,0:T(8,128)(2,1)} %copy-done.5) | copy-start | bytes 3538948
  101.6 2.5 %copy-start.54 = (bf16[394,768]{1,0:T(8,128)(2,1)S(1)}, bf16[394,768]{1,0:T(8,128)(2,1)}, u32[]{:S(2)}) copy-start(bf16[394,768]{1,0:T(8,128)(2,1)} %copy-done.53) | copy-start | bytes 1815556
  104.1 2.3 copy-start
  106.4 40.9 %copy-start.14 = (f32[394,768]{1,0:T(8,128)S(1)}, f32[394,768]{1,0:T(8,128)}, u32[]{:S(2)}) copy-start(f32[394,768]{1,0:T(8,128)} %copy-done.12) | copy-start | bytes 3631108
  151.9 1.9 copy-start.22
  195.6 12.0 %copy-start.48 = (f32[2,6,96]{2,0,1:T(2,128)S(1)}, f32[2,6,96]{2,0,1:T(2,128)}, u32[]{:S(2)}) copy-start(f32[2,6,96]{2,0,1:T(2,128)} %param.33) | copy-start | bytes 13828
  195.6 12.1 %copy-start.44 = (f32[6,96]{1,0:T(8,128)S(1)}, f32[6,96]{1,0:T(8,128)}, u32[]{:S(2)}) copy-start(f32[6,96]{1,0:T(8,128)} %param.26) | copy-start | bytes 6916
  195.6 13.5 %copy-start.39 = (f32[2,12,8]{1,2,0:T(8,128)S(1)}, f32[2,12,8]{1,2,0:T(8,128)}, u32[]{:S(2)}) copy-start(f32[2,12,8]{1,2,0:T(8,128)} %param.32) | copy-start | bytes 2308
  195.6 14.2 %copy-start.49 = (f32[2,2,3,8]{3,1,2,0:T(2,128)S(1)}, f32[2,2,3,8]{3,1,2,0:T(2,128)}, u32[]{:S(2)}) copy-start(f32[2,2,3,8]{3,1,2,0:T(2,128)} %param.31) | copy-start | bytes 1156
  195.6 14.8 %copy-start.29 = (f32[768,96]{0,1:T(8,128)S(1)}, f32[768,96]{0,1:T(8,128)}, u32[]{:S(2)}) copy-start(f32[768,96]{0,1:T(8,128)} %param.23) | copy-start | bytes 884740
  195.6 14.8 %copy-start.35 = (f32[2,768,96]{1,2,0:T(8,128)S(1)}, f32[2,768,96]{1,2,0:T(8,128)}, u32[]{:S(2)}) copy-start(f32[2,768,96]{1,2,0:T(8,128)} %param.30) | copy-start | bytes 1769476
  207.7 4.6 %copy-start.45 = (f32[6,96]{1,0:T(8,128)}, f32[6,96]{1,0:T(8,128)S(1)}, u32[]{:S(2)}) copy-start(f32[6,96]{1,0:T(8,128)S(1)} %get-tuple-element.245) | copy-start | bytes 6916
  218.9 4.4 %copy-start.40 = (f32[12,8]{0,1:T(8,128)}, f32[12,8]{0,1:T(8,128)S(1)}, u32[]{:S(2)}) copy-start(f32[12,8]{0,1:T(8,128)S(1)} %copy.307) | copy-start | bytes 1156
  226.5 3.5 %copy-start.16 = (bf16[394,768]{1,0:T(8,128)(2,1)S(1)}, bf16[394,768]{1,0:T(8,128)(2,1)}, u32[]{:S(2)}) copy-start(bf16[394,768]{1,0:T(8,128)(2,1)} %get-tuple-element.161) | copy-start | bytes 1815556
  (31 other events, 39.9 us)

commit v2 on v1

--- a/solution.py
+++ b/solution.py
@@ -83,7 +83,7 @@
 MESH_ID = pl.DeviceIdType.MESH
 
 
-def exchange(fsdp, tensor, tag, gathers=(), reduces=(), terms=()):
+def exchange(fsdp, tensor, tag, gathers=(), reduces=(), terms=(), shared_rows=0):
     far_n, across_n = fsdp // 2, tensor // 2
     n_g, n_r, n_t = len(gathers), len(reduces), len(terms)
     low = jnp.bfloat16
@@ -99,6 +99,7 @@
         g_out, r_out, t_out = take(n_g), take(n_r), take(n_t)
         r_near, r_sum, r_far = take(n_r), take(n_r), take(n_r)
         t_core, t_half, t_across = take(n_t), take(n_t), take(n_t)
+        peers, p_send, p_recv = take(3) if shared_rows else (None, None, None)
         g_send, g_recv, r_send, r_recv, t_send, t_recv = take(6)
         mine = lax.axis_index("fsdp")
         lane = lax.axis_index("tensor")
@@ -120,9 +121,10 @@
                 pl.semaphore_signal(barrier, inc=1, device_id=(who, lane), device_id_type=MESH_ID)
                 greeted += 1
         if n_t:
-            for who in [mate] + [
-                2 * lax.rem(across + j, across_n) + core for j in range(1, across_n)
-            ]:
+            whom = [mate] + [2 * lax.rem(across + j, across_n) + core for j in range(1, across_n)]
+            if shared_rows:
+                whom = [lax.rem(lane + j, tensor) for j in range(1, tensor)]
+            for who in whom:
                 pl.semaphore_signal(barrier, inc=1, device_id=(mine, who), device_id_type=MESH_ID)
                 greeted += 1
         pl.semaphore_wait(barrier, greeted)
@@ -197,13 +199,34 @@
                         (2 * ahead(j) + near, lane))
                     sent[p, j].start()
                     yield
+            shared = []
             for p in range(n_r):
                 hops[p, 0].wait_recv()
                 total = r_in[p][mine].astype(jnp.float32) + r_near[p][0].astype(jnp.float32)
                 for j in range(1, far_n):
                     sent[p, j].wait_recv()
                     total = total + r_far[p][j - 1].astype(jnp.float32)
+                if p == 0 and shared_rows:
+                    peers[lane] = total
+                    for j in range(1, tensor):
+                        shared.append(
+                            copy(peers.at[lane], peers.at[lane], p_send.at[j], p_recv.at[j],
+                                 (mine, lax.rem(lane + j, tensor))))
+                        shared[-1].start()
+                    yield
                 r_out[p][...] = total
+            for j in range(1, tensor if shared_rows else 1):
+                source = peers.at[lax.rem(lane + tensor - j, tensor)]
+                copy(source, source, p_send.at[j], p_recv.at[j],
+                     (mine, lax.rem(lane + j, tensor))).wait_recv()
+            if shared_rows:
+                total = peers[0]
+                for j in range(1, tensor):
+                    total = total + peers[j]
+                which = lax.broadcasted_iota(jnp.int32, total.shape, 0)
+                r_out[0][...] = jnp.where(which < shared_rows, total, r_out[0][...])
+            for entry in shared:
+                entry.wait_send()
             for entry in list(hops.values()) + list(sent.values()):
                 entry.wait_send()
 
@@ -227,8 +250,8 @@
                         t_half[p], t_across[p].at[j - 1], t_send.at[p, 1 + j], t_recv.at[p, 1 + j],
                         (mine, 2 * lax.rem(across + j, across_n) + core))
                     second[p, j].start()
-            yield
-            yield
+            for _ in range(5 if n_t > 1 else 2):
+                yield
             for p in range(n_t):
                 total = t_half[p][...].astype(jnp.float32)
                 for j in range(1, across_n):
@@ -271,6 +294,12 @@
         + [pltpu.VMEM((a.shape[0], a.shape[1] // 2), low) for a in terms]
         + [pltpu.VMEM((a.shape[0], a.shape[1] // 2), low) for a in terms]
         + [pltpu.VMEM((max(across_n - 1, 1), a.shape[0], a.shape[1] // 2), low) for a in terms]
+        + (
+            [pltpu.VMEM((tensor,) + reduces[0].shape[1:], jnp.float32)]
+            + [pltpu.SemaphoreType.DMA((tensor,))] * 2
+            if shared_rows
+            else []
+        )
         + [pltpu.SemaphoreType.DMA((max(n_g, 1), 2 * far_n))] * 2
         + [pltpu.SemaphoreType.DMA((max(n_r, 1), 2 * far_n))] * 2
         + [pltpu.SemaphoreType.DMA((max(n_t, 1), 1 + across_n))] * 2
@@ -287,6 +316,35 @@
         ),
         name="exchange_" + str(tag),
     )(*args)
+
+
+def step_all(params, grads, moments):
+    count = len(params)
+
+    def kernel(*refs):
+        for p in range(count):
+            param, grad, moment, fresh, copied, moved = refs[p::count]
+            given = grad[...]
+            first = 0.9 * moment[0] + 0.1 * given
+            second = 0.999 * moment[1] + 0.001 * given * given
+            fresh[...] = param[...] - 0.004 * (
+                first / corr_one / (jnp.sqrt(second / corr_two) + 1e-08) + 0.05 * param[...]
+            )
+            copied[...] = given
+            moved[0] = first
+            moved[1] = second
+
+    args = tuple(params) + tuple(grads) + tuple(moments)
+    spec = pl.BlockSpec(memory_space=pltpu.VMEM)
+    outs = pl.pallas_call(
+        kernel,
+        out_shape=tuple(jax.ShapeDtypeStruct(a.shape, a.dtype) for a in args),
+        in_specs=[spec] * len(args),
+        out_specs=tuple([spec] * len(args)),
+        compiler_params=pltpu.CompilerParams(vmem_limit_bytes=48 * 1024 * 1024),
+        name="step_all",
+    )(*args)
+    return outs[:count], outs[count : 2 * count], outs[2 * count :]
 
 
 def row_of(values, lanes):
@@ -359,17 +417,17 @@
         .transpose(1, 2, 0, 3)
         .reshape(2, local_feat)
     )
-    flat = block_input.astype(jnp.float32).reshape(rows, width)
+    flat = block_input.transpose(1, 0, 2).reshape(rows, width).astype(jnp.float32)
     first_norm, unit_one, scale_one = norm_forward(flat, vecf[0], vecf[1])
     normed_one = first_norm.astype(low)
     shifts = jnp.concatenate([biasf[0], jnp.zeros_like(biasf[0]), biasf[1]])
     projected = jnp.dot(normed_one, inward, preferred_element_type=jnp.float32) + shifts
-    triple = projected.astype(low).reshape(images, seqlen, 3, heads_here, HD)
-    queries = triple[:, :, 0]
-    key_rows = triple[:, :, 1]
-    value_rows = triple[:, :, 2]
+    triple = projected.astype(low).reshape(seqlen, images, 3, heads_here, HD)
+    queries = triple[:, :, 0].transpose(1, 0, 2, 3)
+    key_rows = triple[:, :, 1].transpose(1, 0, 2, 3)
+    value_rows = triple[:, :, 2].transpose(1, 0, 2, 3)
     mixed, logsum = attend(queries, key_rows, value_rows)
-    attn_rows = mixed.reshape(rows, local_feat)
+    attn_rows = mixed.transpose(1, 0, 2, 3).reshape(rows, local_feat)
     attn_term = jnp.einsum(
         "nj,dj->nd", attn_rows, outward, preferred_element_type=jnp.float32
     ).astype(low)
@@ -390,10 +448,10 @@
     mlp_term = jnp.einsum(
         "nf,df->nd", activ, narrow, preferred_element_type=jnp.float32
     ).astype(low)
-    row_mask = jnp.broadcast_to(live_images.astype(jnp.float32)[:, None], (images, seqlen)).reshape(
+    row_mask = jnp.broadcast_to(live_images.astype(jnp.float32)[None, :], (seqlen, images)).reshape(
         rows, 1
     )
-    grad_flat = output_grad.astype(jnp.float32).reshape(rows, width) * row_mask
+    grad_flat = output_grad.transpose(1, 0, 2).reshape(rows, width).astype(jnp.float32) * row_mask
     grad_low = grad_flat.astype(low)
     grad_narrow = jnp.einsum("nd,nf->df", grad_low, activ, preferred_element_type=jnp.float32)
     delta_act = jnp.einsum("nd,df->nf", grad_low, narrow, preferred_element_type=jnp.float32)
@@ -421,7 +479,8 @@
     block_output = (
         (row_mask * (resid + mlp_total.astype(jnp.float32) + vecf[5]))
         .astype(low)
-        .reshape(images, seqlen, width)
+        .reshape(seqlen, images, width)
+        .transpose(1, 0, 2)
     )
     delta_resid = grad_flat + norm_backward(delta_two, unit_two, scale_two, vecf[2])
     delta_resid_low = delta_resid.astype(low)
@@ -429,12 +488,18 @@
         "nd,nj->dj", delta_resid_low, attn_rows, preferred_element_type=jnp.float32
     )
     delta_mixed = jnp.dot(delta_resid_low, outward, preferred_element_type=jnp.float32)
-    delta_mixed = delta_mixed.astype(low).reshape(images, seqlen, heads_here, HD)
+    delta_mixed = (
+        delta_mixed.astype(low).reshape(seqlen, images, heads_here, HD).transpose(1, 0, 2, 3)
+    )
     delta_query, delta_key, delta_value = attend_back(
         queries, key_rows, value_rows, logsum, delta_mixed
     )
-    delta_triple = jnp.stack([delta_query, delta_key, delta_value], axis=2).reshape(
-        rows, 3 * local_feat
+    delta_triple = jnp.concatenate(
+        [
+            part.transpose(1, 0, 2, 3).reshape(rows, local_feat)
+            for part in (delta_query, delta_key, delta_value)
+        ],
+        axis=1,
     )
     grad_heads = jnp.stack(
         [
@@ -449,21 +514,10 @@
     one_term = jnp.einsum(
         "nj,dj->nd", triple_low, inward, preferred_element_type=jnp.float32
     ).astype(low)
-    own_inward, own_outward, delta_one = exchange(
-        fsdp,
-        tensor,
-        4,
-        reduces=(blocks(grad_inward), blocks(grad_outward)),
-        terms=(one_term,),
-    )
-    delta_one = delta_one.astype(jnp.float32)
-    input_grad = (delta_resid + norm_backward(delta_one, unit_one, scale_one, vecf[0])).reshape(
-        images, seqlen, width
-    )
     grad_rows_vec = jnp.stack(
         [
-            jnp.sum(delta_one * unit_one, axis=0),
-            jnp.sum(delta_one, axis=0),
+            jnp.sum(one_term.astype(jnp.float32) * unit_one, axis=0),
+            jnp.sum(one_term.astype(jnp.float32), axis=0),
             jnp.sum(delta_two * unit_two, axis=0),
             jnp.sum(delta_two, axis=0),
             jnp.sum(delta_resid, axis=0),
@@ -487,26 +541,64 @@
                 ),
                 lanes,
             ),
+            jnp.zeros((fsdp, small_rows - vec_rows - 2, lanes), jnp.float32),
         ],
         axis=1,
     )
-    (own_small,) = exchange(fsdp, tensor, 5, reduces=(small_grads,))
-    owned = (
-        own_inward.reshape(w_qkv.shape),
-        own_outward.T,
-        own_widen,
-        own_narrow.T,
+    own_small, own_inward, own_outward, delta_one = exchange(
+        fsdp,
+        tensor,
+        4,
+        shared_rows=2,
+        reduces=(small_grads, blocks(grad_inward), blocks(grad_outward)),
+        terms=(one_term,),
+    )
+    delta_one = delta_one.astype(jnp.float32)
+    input_grad = (delta_resid + norm_backward(delta_one, unit_one, scale_one, vecf[0])).reshape(
+        seqlen, images, width
+    ).transpose(1, 0, 2)
+    fresh, given, moved = step_all(
+        (w_qkv.transpose(1, 0, 2), w_out, w_fc1, w_fc2.T),
+        (
+            own_inward.reshape(w_qkv.shape).transpose(1, 0, 2),
+            own_outward.T,
+            own_widen,
+            own_narrow,
+        ),
+        (
+            mom_qkv.transpose(0, 2, 1, 3),
+            mom_out,
+            mom_fc1,
+            mom_fc2.transpose(0, 2, 1),
+        ),
+    )
+    small_owned = (
         own_small[vec_rows + 1, :n_qvb].reshape(qv_bias.shape),
         own_small[vec_rows, :n_fc1b].reshape(fc1_bias.shape),
         own_small[:vec_rows, :owned_rows],
     )
-    params = (w_qkv, w_out, w_fc1, w_fc2, qv_bias, fc1_bias, norm_vec)
-    moments = (mom_qkv, mom_out, mom_fc1, mom_fc2, mom_qvb, mom_fc1b, mom_vec)
-    stepped = [adamw(param, grad, moment) for param, grad, moment in zip(params, owned, moments)]
+    stepped = [
+        adamw(param, grad, moment)
+        for param, grad, moment in zip(
+            (qv_bias, fc1_bias, norm_vec), small_owned, (mom_qvb, mom_fc1b, mom_vec)
+        )
+    ]
+
+    def placed(parts):
+        return (parts[0].transpose(1, 0, 2), parts[1], parts[2], parts[3].T)
+
     return (
         (block_output, input_grad)
-        + tuple(owned)
+        + placed(given)
+        + small_owned
+        + placed(fresh)
         + tuple((entry[0] for entry in stepped))
+        + (
+            moved[0].transpose(0, 2, 1, 3),
+            moved[1],
+            moved[2],
+            moved[3].transpose(0, 2, 1),
+        )
         + tuple((entry[1] for entry in stepped))
     )
 

time: 234 us -> 238 us (1.017)
  local copies, waits for them, and re-layouts: 45 us -> 56.4 us
  Pallas kernels: 136 us -> 131 us
  matrix products: 27.4 us -> 23 us
    unnamed x136 -> x143, local copies, waits for them, and re-layouts: 22.9 us -> 14.1 us
    pallas_call x5 -> x4, Pallas kernels: 136 us -> 128 us  [exchange(): pl.pallas_call(kernel, out_shape=tuple(outs), in_specs=[pl.BlockSpec(memo...]
    another operation x12 -> x5, other arithmetic: 5.07 us -> 1.25 us  [adamw(): return (fresh, jnp.stack([first, second]))]
    convert_element_type x1 -> x3, other arithmetic: 0.01 us -> 3.6 us  [the longest x1 1.44 us: on_device(): output_grad.transpose(1, 0, 2).reshape(rows, width).astype(jnp.float32)]
    convert_element_type x3, local copies, waits for them, and re-layouts: 3.42 us -> 6.84 us  [the longest x1 3.02 us: on_device(): output_grad.transpose(1, 0, 2).reshape(rows, width).astype(jnp.float32)]
    reshape x5 -> x7, local copies, waits for them, and re-layouts: 4.88 us -> 8.2 us  [the longest x1 2.76 us: on_device(): triple = projected.astype(low).reshape(seqlen, images, 3, heads_here, HD)]
    slice x3 -> x2, local copies, waits for them, and re-layouts: 0.02 us -> 2.64 us  [adamw(): second = 0.999 * moments[1] + 0.001 * grad * grad]
    dot_general x1, matrix products: 5.56 us -> 3.17 us  [on_device(): jnp.dot(normed_two, widen, preferred_element_type=jnp.float32) + hidden_bias]
where the time goes in v2:
time: 238 us; the launch traced here: 237 us
  Pallas kernels  131 us (55%)
  local copies, waits for them, and re-layouts  56.4 us (24%)
  other arithmetic  25 us (11%)
  matrix products  23 us (10%)
    pallas_call x4, Pallas kernels, exchange(): pl.pallas_call(kernel, out_shape=tuple(outs), in_specs=[pl.BlockSpec(memo...  128 us
    unnamed x143, local copies, waits for them, and re-layouts  14.1 us

profile of v2, /device:TPU:0, one launch (start us, length us, event | category | flops | bytes accessed | tf_op | source)
XLA Modules:
  0.0 237.3 jit_solution(15644550348700617546)
XLA Ops:
  13.2 1.7 fusion.25
  15.6 2.7 %convert_element_type.183 = bf16[394,768]{1,0:T(8,128)(2,1)} reshape(bf16[197,2,768]{2,1,0:T(2,128)(2,1)} %get-tuple-element.169) | data formatting | bytes 1210368 | tf_op jit(solution)/shard_map/convert_element_type | solution.py:455
  19.7 3.0 %reshape.370 = f32[394,768]{1,0:T(8,128)} reshape(f32[197,2,768]{2,1,0:T(2,128)} %convert_bitcast_fusion) | data formatting | bytes 2420736 | tf_op jit(solution)/shard_map/convert_element_type | solution.py:454
  24.1 3.0 %reshape.369 = f32[394,768]{1,0:T(8,128)} reshape(f32[197,2,768]{2,1,0:T(2,128)} %convert_bitcast_fusion.1) | data formatting | bytes 2420736 | tf_op jit(solution)/shard_map/convert_element_type | solution.py:420
  27.1 26.8 %exchange_1.1 = (bf16[8,16,128]{2,1,0:T(8,128)(2,1)S(1)}, bf16[8,96,576]{2,1,0:T(8,128)(2,1)S(1)}, bf16[8,96,192]{2,1,0:T(8,128)(2,1)S(1)}) custom-call(bf16[16,128]{1,0:T(8,128)(2,1)S(1)} %fusion.79.refs_0_, bf16[96,576]{1,0:T(8,128)(2,1)S(1)} %copy.136.refs_1_, bf16[96,192]{1,0:T(8,128)(2,1)S(1)} %bitcast.167), custom_call_target="tpu_custom_call" | custom-call | tf_op jit(solution)/shard_map/exchange_1/pallas_call | solution.py:308
  58.2 1.9 add_convert_fusion.2
  60.1 2.0 convert_element_type.166
  62.1 2.1 fusion.3
  64.2 2.8 %reshape.350 = bf16[197,2,3,3,64]{4,3,2,1,0:T(4,128)(2,1)S(1)} reshape(bf16[394,576]{1,0:T(8,128)(2,1)} %fusion.3) | data formatting | bytes 907776 | tf_op jit(solution)/shard_map/reshape | solution.py:425
  73.8 33.9 %exchange_2.1 = (bf16[8,96,768]{2,1,0:T(8,128)(2,1)S(1)}, bf16[8,96,768]{2,1,0:T(8,128)(2,1)S(1)}, bf16[394,768]{1,0:T(8,128)(2,1)S(1)}) custom-call(bf16[96,768]{1,0:T(8,128)(2,1)S(1)} %convert_element_type.159.refs_0_, bf16[96,768]{1,0:T(8,128)(2,1)S(1)} %convert_bitcast_fusion.4.refs_1_, bf16[394,768]{1,0:T(8,128)(2,1)S(1)} %convolution_convert_fusion.6.refs_2_), custom_call_target="tpu_custom_call" | custom-call | tf_op jit(solution)/shard_map/exchange_2/pallas_call | solution.py:308
  108.8 3.2 %fusion.11 = (bf16[394,768]{1,0:T(8,128)(2,1)S(1)}, f32[394,768]{1,0:T(8,128)S(1)}) fusion(f32[768]{0:T(1024)S(1)} %copy-done.63, bf16[768,768]{1,0:T(8,128)(2,1)S(1)} %bitcast.168, f32[394,768]{1,0:T(8,128)S(1)} %get-tuple-element.163, f32[768]{0:T(1024)S(1)} %copy-done.62, f32[768]{0:T(1024)S(1)} %mul.403, f32[394]{0:T(512)S(1)} %add_rsqrt_fusion.1, ...), kind=kOutput, calls=%fused_computation.31 | convolution fusion | flops 486265344 | bytes 4217936 | tf_op jit(solution)/shard_map/dot_general | solution.py:446
  114.6 2.3 convolution_convert_fusion.1
  118.0 36.1 %exchange_3.1 = (f32[96,768]{1,0:T(8,128)S(1)}, f32[96,768]{1,0:T(8,128)S(1)}, bf16[394,768]{1,0:T(8,128)(2,1)S(1)}, bf16[394,768]{1,0:T(8,128)(2,1)S(1)}) custom-call(bf16[8,96,768]{2,1,0:T(8,128)(2,1)S(1)} %bitcast.159, bf16[8,96,768]{2,1,0:T(8,128)(2,1)S(1)} %bitcast.160, bf16[394,768]{1,0:T(8,128)(2,1)S(1)} %convolution_convert_fusion.5.refs_2_, ...), custom_call_target="tpu_custom_call" | custom-call | tf_op jit(solution)/shard_map/exchange_3/pallas_call | solution.py:308
  156.8 2.3 fusion.90
  161.2 1.7 convolution_convert_fusion.7
  163.1 1.9 reshape.358
  165.0 1.9 copy.146
  176.5 2.3 convert_reduce_fusion.1
  179.1 3.2 %convolution_convert_fusion.2 = bf16[768,576]{0,1:T(8,128)(2,1)} fusion(f32[394,768]{1,0:T(8,128)} %reshape.369, f32[768]{0:T(1024)S(1)} %copy-done.52, f32[768]{0:T(1024)S(1)} %mul.395, f32[394]{0:T(512)S(1)} %div.77, f32[394]{0:T(512)S(1)} %copy-done.49, bf16[394,192]{1,0:T(8,128)(2,1)S(1)} %copy-done.41, bf16[394,192]{1,0:T(8,128)(2,1)S(1)} %copy-done.42, ...), kind=kOutput, calls=%fused_computation.14 | convolution fusion | flops 351902976 | bytes 2558288 | tf_op jit(solution)/shard_map/nd,nj->dj/dot_general | solution.py:511
  183.8 31.6 %exchange_4.1 = (f32[16,128]{1,0:T(8,128)S(1)}, f32[96,576]{1,0:T(8,128)S(1)}, f32[96,192]{1,0:T(8,128)S(1)}, bf16[394,768]{1,0:T(8,128)(2,1)S(1)}) custom-call(f32[8,16,128]{2,1,0:T(8,128)S(1)} %fusion.52.refs_0_, bf16[8,96,576]{2,1,0:T(8,128)(2,1)S(1)} %bitcast.155, bf16[8,96,192]{2,1,0:T(8,128)(2,1)S(1)} %bitcast.158, ...), custom_call_target="tpu_custom_call" | custom-call | tf_op jit(solution)/shard_map/exchange_4/pallas_call | solution.py:308
  221.5 1.8 fusion.17
  223.3 2.8 %multiply_add_fusion = f32[394,768]{1,0:T(8,128)} fusion(f32[394,768]{1,0:T(8,128)} %copy-done.24, bf16[394,768]{1,0:T(8,128)(2,1)S(1)} %get-tuple-element.57, f32[394,768]{1,0:T(8,128)S(1)} %copy-done.23, f32[394]{0:T(512)S(1)} %broadcast_multiply_fusion.1, f32[394]{0:T(512)S(1)} %broadcast_multiply_fusion.2, f32[768]{0:T(1024)S(1)} %copy-done.44, ...), kind=kLoop, calls=%fused_computation.37 | loop fusion | flops 2723328 | bytes 4245664 | tf_op jit(solution)/shard_map/add | solution.py:557
  226.1 3.0 %reshape.367 = f32[197,2,768]{2,1,0:T(2,128)} reshape(f32[394,768]{1,0:T(8,128)} %multiply_add_fusion) | data formatting | bytes 2420736 | tf_op jit(solution)/shard_map/reshape | solution.py:557
  234.8 2.3 step_all.1
  (268 shorter events, 59.1 us)
Async XLA Ops:
  0.7 10.1 %copy-start.27 = (bf16[2,197,768]{2,0,1:T(2,128)(2,1)S(1)}, bf16[2,197,768]{2,0,1:T(2,128)(2,1)}, u32[]{:S(2)}) copy-start(bf16[2,197,768]{2,0,1:T(2,128)(2,1)} %param.17) | copy-start | bytes 1815556
  7.2 5.6 %copy-start = (f32[96,3,192]{2,0,1:T(8,128)S(1)}, f32[96,3,192]{2,0,1:T(8,128)}, u32[]{:S(2)}) copy-start(f32[96,3,192]{2,0,1:T(8,128)} %param.20) | copy-start | bytes 663556
  10.8 168.3 %copy-start.47 = (f32[394]{0:T(512)}, f32[394]{0:T(512)S(1)}, u32[]{:S(2)}) copy-start(f32[394]{0:T(512)S(1)} %div.77) | copy-start | bytes 4732
  53.9 8.1 %copy-start.18 = (bf16[8,96,576]{2,1,0:T(8,128)(2,1)}, bf16[8,96,576]{2,1,0:T(8,128)(2,1)S(1)}, u32[]{:S(2)}) copy-start(bf16[8,96,576]{2,1,0:T(8,128)(2,1)S(1)} %get-tuple-element.50) | copy-start | bytes 2654212
  55.0 124.0 %copy-start.43 = (f32[768]{0:T(1024)}, f32[768]{0:T(1024)S(1)}, u32[]{:S(2)}) copy-start(f32[768]{0:T(1024)S(1)} %mul.395) | copy-start | bytes 9220
  73.2 34.6 %copy-start.22 = (f32[394,768]{1,0:T(8,128)S(1)}, f32[394,768]{1,0:T(8,128)}, u32[]{:S(2)}) copy-start(f32[394,768]{1,0:T(8,128)} %reshape.369) | copy-start | bytes 3631108
  73.2 34.6 %copy-start.53 = (f32[768]{0:T(1024)S(1)}, f32[768]{0:T(1024)}, u32[]{:S(2)}) copy-start(f32[768]{0:T(1024)} %add.184) | copy-start | bytes 9220
  73.5 34.6 %copy-start.29 = (bf16[394,192]{1,0:T(8,128)(2,1)}, bf16[394,192]{1,0:T(8,128)(2,1)S(1)}, u32[]{:S(2)}) copy-start(bf16[394,192]{1,0:T(8,128)(2,1)S(1)} %reshape.351) | copy-start | bytes 453892
  163.0 5.4 %copy-start.21 = (f32[2,3,197,197]{2,3,1,0:T(8,128)S(1)}, f32[2,3,197,197]{2,3,1,0:T(8,128)}, u32[]{:S(2)}) copy-start(f32[2,3,197,197]{2,3,1,0:T(8,128)} %copy-done.20) | copy-start | bytes 2794252
  163.0 5.4 %copy-start.34 = (bf16[197,2,1,3,64]{0,4,3,1,2:T(8,128)(2,1)S(1)}, bf16[197,2,1,3,64]{0,4,3,1,2:T(8,128)(2,1)}, u32[]{:S(2)}) copy-start(bf16[197,2,1,3,64]{0,4,3,1,2:T(8,128)(2,1)} %copy-done.33) | copy-start | bytes 453892
  183.8 33.1 %copy-start.46 = (f32[1,6,96]{2,0,1:T(1,128)S(1)}, f32[1,6,96]{2,0,1:T(1,128)}, u32[]{:S(2)}) copy-start(f32[1,6,96]{2,0,1:T(1,128)} %get-tuple-element.185) | copy-start | bytes 6916
  183.8 33.1 %copy-start.57 = (f32[6,96]{1,0:T(8,128)S(1)}, f32[6,96]{1,0:T(8,128)}, u32[]{:S(2)}) copy-start(f32[6,96]{1,0:T(8,128)} %param.26) | copy-start | bytes 6916
  183.8 33.1 %copy-start.60 = (f32[1,6,96]{2,0,1:T(1,128)S(1)}, f32[1,6,96]{2,0,1:T(1,128)}, u32[]{:S(2)}) copy-start(f32[1,6,96]{2,0,1:T(1,128)} %get-tuple-element.184) | copy-start | bytes 6916
  216.8 6.5 %copy-start.23 = (f32[394,768]{1,0:T(8,128)S(1)}, f32[394,768]{1,0:T(8,128)}, u32[]{:S(2)}) copy-start(f32[394,768]{1,0:T(8,128)} %reshape.369) | copy-start | bytes 3631108
  216.8 6.5 %copy-start.44 = (f32[768]{0:T(1024)S(1)}, f32[768]{0:T(1024)}, u32[]{:S(2)}) copy-start(f32[768]{0:T(1024)} %copy-done.43) | copy-start | bytes 9220
  216.8 6.5 %copy-start.48 = (f32[394]{0:T(512)S(1)}, f32[394]{0:T(512)}, u32[]{:S(2)}) copy-start(f32[394]{0:T(512)} %copy-done.47) | copy-start | bytes 4732
  216.8 6.5 %copy-start.50 = (f32[394]{0:T(512)S(1)}, f32[394]{0:T(512)}, u32[]{:S(2)}) copy-start(f32[394]{0:T(512)} %rsqrt.22) | copy-start | bytes 4732
  216.9 9.2 %copy-start.58 = (f32[6,96]{1,0:T(8,128)}, f32[6,96]{1,0:T(8,128)S(1)}, u32[]{:S(2)}) copy-start(f32[6,96]{1,0:T(8,128)S(1)} %get-tuple-element.159) | copy-start | bytes 6916
  226.1 4.0 %copy-start.56 = (f32[12,8]{0,1:T(8,128)S(1)}, f32[12,8]{0,1:T(8,128)}, u32[]{:S(2)}) copy-start(f32[12,8]{0,1:T(8,128)} %param.25) | copy-start | bytes 1156
  226.1 4.6 %copy-start.14 = (f32[96,576]{1,0:T(8,128)S(1)}, f32[96,576]{1,0:T(8,128)}, u32[]{:S(2)}) copy-start(f32[96,576]{1,0:T(8,128)} %copy-done.13) | copy-start | bytes 663556
  226.1 6.6 %copy-start.17 = (f32[96,192]{1,0:T(8,128)S(1)}, f32[96,192]{1,0:T(8,128)}, u32[]{:S(2)}) copy-start(f32[96,192]{1,0:T(8,128)} %copy-done.16) | copy-start | bytes 221188
  226.1 6.7 %copy-start.7 = (f32[2,768,96]{1,2,0:T(8,128)S(1)}, f32[2,768,96]{1,2,0:T(8,128)}, u32[]{:S(2)}) copy-start(f32[2,768,96]{1,2,0:T(8,128)} %param.30) | copy-start | bytes 1769476
  226.1 6.7 %copy-start.10 = (f32[96,768]{1,0:T(8,128)S(1)}, f32[96,768]{1,0:T(8,128)}, u32[]{:S(2)}) copy-start(f32[96,768]{1,0:T(8,128)} %copy-done.9) | copy-start | bytes 884740
  230.1 7.0 %copy-start.55 = (f32[12,8]{0,1:T(8,128)}, f32[12,8]{0,1:T(8,128)S(1)}, u32[]{:S(2)}) copy-start(f32[12,8]{0,1:T(8,128)S(1)} %copy.180) | copy-start | bytes 1156
  (43 other events, 80.8 us)
